TPU v7x, 256 devices: a whole 4x4x8 slice. The times are simulated.
256 devices in a mesh: obs: 8 (over z_hi, core), gx: 8 (over y, z_lo), gy: 4 (over x).
Axes of the slice: x: 4, y: 4, z: 8 (z_hi: 4, z_lo: 2; z = z_hi * 2 + z_lo), core: 2. Of those that a mesh axis runs over, the one named last changes fastest.
Arguments:
- closing_costates: float32 [2, 32, 64, 64, 128], P(None, 'obs', 'gx', 'gy'), may hold values from -6.5 to 6.5
- saved_pore_load: float32 [3, 64, 64, 128], P(None, 'gx', 'gy', 'obs'), may hold values from -4 to 4
- saved_heat_field: float32 [3, 64, 64, 128], P(None, 'gx', 'gy', 'obs'), may hold values from -2.5 to -0.5
- saved_dilatation: float32 [3, 64, 64, 128], P(None, 'gx', 'gy', 'obs'), may hold values from -2.5 to -0.5
- saved_conductivity: float32 [3, 64, 64, 128], P(None, 'gx', 'gy', 'obs'), may hold values from 2.5 to 5
- data_residual: float32 [3, 32, 128], P(None, 'obs'), may hold values from -8 to 8
- borehole_flat_position: int32 [32], P('obs'), may hold values from 0 to 4095
- probe_multiplier: int32 [32], P('obs'), may hold values from 1 to 4
Outputs:
- adjoint_start: float32 [2, 32, 64, 64, 128], P(None, 'obs', 'gx', 'gy')
- gradient: float32 [64, 64, 128], P('gx', 'gy', 'obs')
All inputs are finite; a program needn't handle non-finite values.
Results may differ from a plain program's by a relative error of at most 0.0003.
Values sent between devices are 32-bit elements; how exact they have to be, the bound alone decides.
A program may use at most 64 MiB of HBM per device.

v0:
```python
import jax
import jax.numpy as jnp
from jax import lax
from jax.sharding import PartitionSpec as P

ITERS = 4


heat_diffusivity = 2.0


def padded_2(value, sides, width):
    for axis, dim in sides:
        count, length = (lax.axis_size(axis), value.shape[dim])
        up = [(i, (i + 1) % count) for i in range(count - 1)]
        down = [(j, i) for i, j in up]
        last = lax.slice_in_dim(value, length - width, length, axis=dim)
        initial = lax.slice_in_dim(value, 0, width, axis=dim)
        before = lax.ppermute(last, axis, up)
        after = lax.ppermute(initial, axis, down)
        value = jnp.concatenate([before, value, after], axis=dim)
    return value


def neighbour_sum(padded):
    centre = padded[..., 1:-1, 1:-1, :]
    widths = [(0, 0)] * (centre.ndim - 1) + [(1, 1)]
    deeper = jnp.pad(centre, widths)
    summed = padded[..., 2:, 1:-1, :] + padded[..., :-2, 1:-1, :]
    summed = summed + padded[..., 1:-1, 2:, :] + padded[..., 1:-1, :-2, :]
    return summed + deeper[..., 2:] + deeper[..., :-2]


def whole_faces(costate_vector):
    return padded_2(costate_vector, (("gx", 2), ("gy", 3)), 1)


def relax_group(costate_vector, rights, coeffs):
    perm_now, coupling, diag_p, heat_main_entry = coeffs
    padded = whole_faces(costate_vector)
    near = neighbour_sum(padded)
    new_p = (rights[0] + perm_now * near[0] + coupling * costate_vector[1]) / diag_p
    new_t = (rights[1] + heat_diffusivity * near[1] + coupling * new_p) / heat_main_entry
    return jnp.stack([new_p, new_t])


def local(
    closing_costates,
    saved_pore_load,
    saved_heat_field,
    saved_dilatation,
    saved_conductivity,
    data_residual,
    borehole_flat_position,
    probe_multiplier,
):
    step_count = saved_pore_load.shape[0]
    cells_x = closing_costates.shape[2]
    cells_y = closing_costates.shape[3]
    full_y = cells_y * lax.axis_size("gy")
    rows_x = lax.axis_index("gx") * cells_x + jnp.arange(cells_x, dtype=jnp.int32)
    cols_y = lax.axis_index("gy") * cells_y + jnp.arange(cells_y, dtype=jnp.int32)
    flat_index = rows_x[:, None] * full_y + cols_y[None, :]
    well_mask = (flat_index[None] == borehole_flat_position[:, None, None]).astype(jnp.float32)[
        ..., None
    ]
    weights = probe_multiplier.astype(jnp.float32)
    costate_vector = closing_costates
    gradient_shard = jnp.zeros(saved_pore_load.shape[1:], jnp.float32)
    for backward_counter in range(step_count - 1, -1, -1):
        pressure_now, present_heat_field, strain_now, perm_now = (
            lax.all_gather(saved_pore_load[backward_counter], "obs", axis=2, tiled=True),
            lax.all_gather(saved_heat_field[backward_counter], "obs", axis=2, tiled=True),
            lax.all_gather(saved_dilatation[backward_counter], "obs", axis=2, tiled=True),
            lax.all_gather(saved_conductivity[backward_counter], "obs", axis=2, tiled=True),
        )
        store_p = jnp.exp(strain_now)
        kept_heat_field = jnp.exp(0.5 * present_heat_field)
        coupling = 0.2 * jnp.tanh(pressure_now)
        diag_p = store_p + 6.0 * perm_now
        heat_main_entry = kept_heat_field + 6.0 * heat_diffusivity
        coeffs = (perm_now, coupling, diag_p, heat_main_entry)
        right_p = (
            store_p * costate_vector[0]
            + well_mask * data_residual[backward_counter][:, None, None, :]
        )
        heat_source_term = kept_heat_field * costate_vector[1]
        rights = jnp.stack([right_p, heat_source_term])
        for sweep_index in range(ITERS):
            costate_vector = relax_group(costate_vector, rights, coeffs)
        padded_p = padded_2(pressure_now, (("gx", 0), ("gy", 1)), 1)
        laplace = neighbour_sum(padded_p) - 6.0 * pressure_now
        weighted = jnp.sum(weights[:, None, None, None] * costate_vector[0], axis=0)
        grad_term = perm_now * laplace * weighted
        gradient_shard = gradient_shard + lax.psum_scatter(
            grad_term, "obs", scatter_dimension=2, tiled=True
        )
    return (costate_vector, gradient_shard)


def solution(mesh):
    return jax.shard_map(
        local,
        mesh=mesh,
        in_specs=(
            P(None, "obs", "gx", "gy", None),
            P(None, "gx", "gy", "obs"),
            P(None, "gx", "gy", "obs"),
            P(None, "gx", "gy", "obs"),
            P(None, "gx", "gy", "obs"),
            P(None, "obs", None),
            P("obs"),
            P("obs"),
        ),
        out_specs=(P(None, "obs", "gx", "gy", None), P("gx", "gy", "obs")),
        check_vma=False,
    )
```

profile of v0, /device:TPU:1, one launch (start us, length us, event | category | flops | bytes accessed | tf_op | source)
XLA Modules:
  0.0 512.6 jit_solution(1496356348282304289)
XLA Ops:
  9.4 5.0 collective-permute-start.1
  14.6 19.5 %all-gather.4 = f32[1,8,16,128]{2,1,0,3:T(8,128)S(1)} all-gather(f32[1,8,16,16]{2,1,0,3:T(8,128)S(1)} %copy.160), channel_id=6, replica_groups=mesh['obs'=8,'gx'=8,'gy'=4] {'obs'}, dimensions={3}, use_global_device_ids=true | all-gather | bytes 73728 | tf_op jit(solution)/shard_map/all_gather | solution.py:72
  36.1 5.3 %collective-permute-start.49 = (f32[1,16,128]{1,2,0:T(8,128)}, f32[1,16,128]{1,2,0:T(8,128)}, u32[]{:S(2)}, u32[]{:S(2)}) collective-permute-start(f32[1,16,128]{1,2,0:T(8,128)} %bitcast.18), channel_id=1, source_target_pairs={{0,4},{4,8},{8,12},{12,16},{16,20},{20,24},{24,28},{1,5},{5,9},{9,... | collective-permute-start | bytes 24584 | tf_op jit(solution)/shard_map/ppermute | solution.py:19
  41.4 15.5 %all-gather.7 = f32[1,8,16,128]{2,1,0,3:T(8,128)S(1)} all-gather(f32[1,8,16,16]{2,1,0,3:T(8,128)S(1)} %copy.163), channel_id=9, replica_groups=mesh['obs'=8,'gx'=8,'gy'=4] {'obs'}, dimensions={3}, use_global_device_ids=true | all-gather | bytes 73728 | tf_op jit(solution)/shard_map/all_gather | solution.py:72
  60.6 15.2 %all-gather.5 = f32[1,8,16,128]{2,1,0,3:T(8,128)S(1)} all-gather(f32[1,8,16,16]{2,1,0,3:T(8,128)S(1)} %copy.161), channel_id=7, replica_groups=mesh['obs'=8,'gx'=8,'gy'=4] {'obs'}, dimensions={3}, use_global_device_ids=true | all-gather | bytes 73728 | tf_op jit(solution)/shard_map/all_gather | solution.py:73
  78.3 15.1 %all-gather.10 = f32[1,8,16,128]{2,1,0,3:T(8,128)S(1)} all-gather(f32[1,8,16,16]{2,1,0,3:T(8,128)S(1)} %copy.166), channel_id=12, replica_groups=mesh['obs'=8,'gx'=8,'gy'=4] {'obs'}, dimensions={3}, use_global_device_ids=true | all-gather | bytes 73728 | tf_op jit(solution)/shard_map/all_gather | solution.py:72
  94.3 15.0 %all-gather.3 = f32[1,8,16,128]{2,1,0,3:T(8,128)S(1)} all-gather(f32[1,8,16,16]{2,1,0,3:T(8,128)S(1)} %copy.159), channel_id=5, replica_groups=mesh['obs'=8,'gx'=8,'gy'=4] {'obs'}, dimensions={3}, use_global_device_ids=true | all-gather | bytes 73728 | tf_op jit(solution)/shard_map/all_gather | solution.py:75
  109.4 15.2 %all-gather.6 = f32[1,8,16,128]{2,1,0,3:T(8,128)S(1)} all-gather(f32[1,8,16,16]{2,1,0,3:T(8,128)S(1)} %copy.162), channel_id=8, replica_groups=mesh['obs'=8,'gx'=8,'gy'=4] {'obs'}, dimensions={3}, use_global_device_ids=true | all-gather | bytes 73728 | tf_op jit(solution)/shard_map/all_gather | solution.py:75
  124.8 15.2 %all-gather.9 = f32[1,8,16,128]{2,1,0,3:T(8,128)S(1)} all-gather(f32[1,8,16,16]{2,1,0,3:T(8,128)S(1)} %copy.165), channel_id=11, replica_groups=mesh['obs'=8,'gx'=8,'gy'=4] {'obs'}, dimensions={3}, use_global_device_ids=true | all-gather | bytes 73728 | tf_op jit(solution)/shard_map/all_gather | solution.py:75
  140.1 15.2 %all-gather.2 = f32[1,8,16,128]{2,1,0,3:T(8,128)S(1)} all-gather(f32[1,8,16,16]{2,1,0,3:T(8,128)S(1)} %copy.158), channel_id=4, replica_groups=mesh['obs'=8,'gx'=8,'gy'=4] {'obs'}, dimensions={3}, use_global_device_ids=true | all-gather | bytes 73728 | tf_op jit(solution)/shard_map/all_gather | solution.py:74
  155.6 15.2 %all-gather.1 = f32[1,8,16,128]{2,1,0,3:T(8,128)S(1)} all-gather(f32[1,8,16,16]{2,1,0,3:T(8,128)S(1)} %copy.157), channel_id=3, replica_groups=mesh['obs'=8,'gx'=8,'gy'=4] {'obs'}, dimensions={3}, use_global_device_ids=true | all-gather | bytes 73728 | tf_op jit(solution)/shard_map/all_gather | solution.py:74
  170.9 15.1 %all-gather = f32[1,8,16,128]{2,1,0,3:T(8,128)S(1)} all-gather(f32[1,8,16,16]{2,1,0,3:T(8,128)S(1)} %copy.156), channel_id=2, replica_groups=mesh['obs'=8,'gx'=8,'gy'=4] {'obs'}, dimensions={3}, use_global_device_ids=true | all-gather | bytes 73728 | tf_op jit(solution)/shard_map/all_gather | solution.py:74
  201.2 16.4 %all-gather.8 = f32[1,8,16,128]{2,1,0,3:T(8,128)S(1)} all-gather(f32[1,8,16,16]{2,1,0,3:T(8,128)S(1)} %copy.164), channel_id=10, replica_groups=mesh['obs'=8,'gx'=8,'gy'=4] {'obs'}, dimensions={3}, use_global_device_ids=true | all-gather | bytes 73728 | tf_op jit(solution)/shard_map/all_gather | solution.py:73
  219.2 4.6 collective-permute-start.7
  225.5 7.3 %collective-permute-start.9 = (f32[2,4,1,16,128]{4,3,2,1,0:T(8,128)S(1)}, f32[2,4,1,16,128]{4,3,2,1,0:T(8,128)S(1)}, u32[]{:S(2)}, u32[]{:S(2)}) collective-permute-start(f32[2,4,1,16,128]{4,3,2,1,0:T(8,128)S(1)} %get-tuple-element.79), channel_id=1, source_target_pairs={{0,4},{4,8},{8,12},{12,16},{16,20},{20,24},{24,28},{1,5},{5,9},{9,... | collective-permute-start | bytes 196616 | tf_op jit(solution)/shard_map/ppermute | solution.py:19
  240.4 4.6 collective-permute-start.11
  287.0 25.5 %all-gather.11 = f32[1,8,16,128]{2,1,0,3:T(8,128)} all-gather(f32[1,8,16,16]{2,1,0,3:T(8,128)} %copy.167), channel_id=13, replica_groups=mesh['obs'=8,'gx'=8,'gy'=4] {'obs'}, dimensions={3}, use_global_device_ids=true | all-gather | bytes 73728 | tf_op jit(solution)/shard_map/all_gather | solution.py:73
  316.5 4.6 collective-permute-start.23
  362.9 4.6 collective-permute-start.53
  385.2 5.2 %collective-permute-start.57 = (f32[1,16,128]{1,2,0:T(8,128)}, f32[1,16,128]{1,2,0:T(8,128)}, u32[]{:S(2)}, u32[]{:S(2)}) collective-permute-start(f32[1,16,128]{1,2,0:T(8,128)} %bitcast.39), channel_id=1, source_target_pairs={{0,4},{4,8},{8,12},{12,16},{16,20},{20,24},{24,28},{1,5},{5,9},{9,... | collective-permute-start | bytes 24584 | tf_op jit(solution)/shard_map/ppermute | solution.py:19
  396.1 5.3 %collective-permute-start.39 = (f32[2,4,10,1,128]{4,3,2,1,0:T(1,128)S(1)}, f32[2,4,10,1,128]{4,3,2,1,0:T(1,128)S(1)}, u32[]{:S(2)}, u32[]{:S(2)}) collective-permute-start(f32[2,4,10,1,128]{4,3,2,1,0:T(1,128)S(1)} %get-tuple-element.36), channel_id=1, source_target_pairs={{0,1},{1,2},{2,3},{4,5},{5,6},{6,7},{8,9},{9,10},{10,11},{12,13},{... | collective-permute-start | bytes 122888 | tf_op jit(solution)/shard_map/ppermute | solution.py:19
  419.9 4.6 collective-permute-start.43
  437.0 4.7 collective-permute-start.47
  457.6 46.6 %reduce-scatter.4.cloned.1.call-done = f32[16,128]{1,0:T(8,128)} async-done(((f32[128,128]{1,0:T(8,128)}), f32[16,128]{1,0:T(8,128)}) %reduce-scatter.4.cloned.1.call-update) | async-done | bytes 8208
  (464 shorter events, 195.5 us)
Async XLA Ops:
  7.2 497.1 %reduce-scatter.4.cloned.1.call-start = ((), (), s32[]{:S(2)}) async-start(), calls=%async_computation.1 | async-start | bytes 73728
  8.1 179.7 %collective-permute-start = (f32[2,4,1,16,128]{4,3,2,1,0:T(8,128)S(1)}, f32[2,4,1,16,128]{4,3,2,1,0:T(8,128)S(1)}, u32[]{:S(2)}, u32[]{:S(2)}) collective-permute-start(f32[2,4,1,16,128]{4,3,2,1,0:T(8,128)S(1)} %get-tuple-element.83), channel_id=1, source_target_pairs={{4,0},{8,4},{12,8},{16,12},{20,16},{24,20},{28,24},{5,1},{9,5},{13... | collective-permute-start | bytes 196616 | tf_op jit(solution)/shard_map/ppermute | solution.py:20
  9.4 178.3 %collective-permute-start.1 = (f32[2,4,1,16,128]{4,3,2,1,0:T(8,128)S(1)}, f32[2,4,1,16,128]{4,3,2,1,0:T(8,128)S(1)}, u32[]{:S(2)}, u32[]{:S(2)}) collective-permute-start(f32[2,4,1,16,128]{4,3,2,1,0:T(8,128)S(1)} %get-tuple-element.84), channel_id=1, source_target_pairs={{0,4},{4,8},{8,12},{12,16},{16,20},{20,24},{24,28},{1,5},{5,9},{9,... | collective-permute-start | bytes 196616 | tf_op jit(solution)/shard_map/ppermute | solution.py:19
  34.8 328.1 %collective-permute-start.48 = (f32[1,16,128]{1,2,0:T(8,128)}, f32[1,16,128]{1,2,0:T(8,128)}, u32[]{:S(2)}, u32[]{:S(2)}) collective-permute-start(f32[1,16,128]{1,2,0:T(8,128)} %bitcast.17), channel_id=1, source_target_pairs={{4,0},{8,4},{12,8},{16,12},{20,16},{24,20},{28,24},{5,1},{9,5},{13... | collective-permute-start | bytes 24584 | tf_op jit(solution)/shard_map/ppermute | solution.py:20
  36.1 332.3 %collective-permute-start.49 = (f32[1,16,128]{1,2,0:T(8,128)}, f32[1,16,128]{1,2,0:T(8,128)}, u32[]{:S(2)}, u32[]{:S(2)}) collective-permute-start(f32[1,16,128]{1,2,0:T(8,128)} %bitcast.18), channel_id=1, source_target_pairs={{0,4},{4,8},{8,12},{12,16},{16,20},{20,24},{24,28},{1,5},{5,9},{9,... | collective-permute-start | bytes 24584 | tf_op jit(solution)/shard_map/ppermute | solution.py:19
  57.7 327.6 %collective-permute-start.52 = (f32[1,16,128]{1,2,0:T(8,128)}, f32[1,16,128]{1,2,0:T(8,128)}, u32[]{:S(2)}, u32[]{:S(2)}) collective-permute-start(f32[1,16,128]{1,2,0:T(8,128)} %bitcast.28), channel_id=1, source_target_pairs={{4,0},{8,4},{12,8},{16,12},{20,16},{24,20},{28,24},{5,1},{9,5},{13... | collective-permute-start | bytes 24584 | tf_op jit(solution)/shard_map/ppermute | solution.py:20
  195.4 22.4 %collective-permute-start.5 = (f32[2,4,1,16,128]{4,3,2,1,0:T(8,128)S(1)}, f32[2,4,1,16,128]{4,3,2,1,0:T(8,128)S(1)}, u32[]{:S(2)}, u32[]{:S(2)}) collective-permute-start(f32[2,4,1,16,128]{4,3,2,1,0:T(8,128)S(1)} %get-tuple-element.81), channel_id=1, source_target_pairs={{0,4},{4,8},{8,12},{12,16},{16,20},{20,24},{24,28},{1,5},{5,9},{9,... | collective-permute-start | bytes 196616 | tf_op jit(solution)/shard_map/ppermute | solution.py:19
  199.2 18.6 %collective-permute-start.4 = (f32[2,4,1,16,128]{4,3,2,1,0:T(8,128)S(1)}, f32[2,4,1,16,128]{4,3,2,1,0:T(8,128)S(1)}, u32[]{:S(2)}, u32[]{:S(2)}) collective-permute-start(f32[2,4,1,16,128]{4,3,2,1,0:T(8,128)S(1)} %get-tuple-element.82), channel_id=1, source_target_pairs={{4,0},{8,4},{12,8},{16,12},{20,16},{24,20},{28,24},{5,1},{9,5},{13... | collective-permute-start | bytes 196616 | tf_op jit(solution)/shard_map/ppermute | solution.py:20
  225.5 9.3 %collective-permute-start.9 = (f32[2,4,1,16,128]{4,3,2,1,0:T(8,128)S(1)}, f32[2,4,1,16,128]{4,3,2,1,0:T(8,128)S(1)}, u32[]{:S(2)}, u32[]{:S(2)}) collective-permute-start(f32[2,4,1,16,128]{4,3,2,1,0:T(8,128)S(1)} %get-tuple-element.79), channel_id=1, source_target_pairs={{0,4},{4,8},{8,12},{12,16},{16,20},{20,24},{24,28},{1,5},{5,9},{9,... | collective-permute-start | bytes 196616 | tf_op jit(solution)/shard_map/ppermute | solution.py:19
  279.6 34.8 %collective-permute-start.21 = (f32[2,4,1,16,128]{4,3,2,1,0:T(8,128)}, f32[2,4,1,16,128]{4,3,2,1,0:T(8,128)}, u32[]{:S(2)}, u32[]{:S(2)}) collective-permute-start(f32[2,4,1,16,128]{4,3,2,1,0:T(8,128)} %get-tuple-element.73), channel_id=1, source_target_pairs={{0,4},{4,8},{8,12},{12,16},{16,20},{20,24},{24,28},{1,5},{5,9},{9,... | collective-permute-start | bytes 196616 | tf_op jit(solution)/shard_map/ppermute | solution.py:19
  283.5 30.8 %collective-permute-start.20 = (f32[2,4,1,16,128]{4,3,2,1,0:T(8,128)}, f32[2,4,1,16,128]{4,3,2,1,0:T(8,128)}, u32[]{:S(2)}, u32[]{:S(2)}) collective-permute-start(f32[2,4,1,16,128]{4,3,2,1,0:T(8,128)} %get-tuple-element.74), channel_id=1, source_target_pairs={{4,0},{8,4},{12,8},{16,12},{20,16},{24,20},{28,24},{5,1},{9,5},{13... | collective-permute-start | bytes 196616 | tf_op jit(solution)/shard_map/ppermute | solution.py:20
  358.1 12.5 %collective-permute-start.33 = (f32[2,4,1,16,128]{4,3,2,1,0:T(8,128)S(1)}, f32[2,4,1,16,128]{4,3,2,1,0:T(8,128)S(1)}, u32[]{:S(2)}, u32[]{:S(2)}) collective-permute-start(f32[2,4,1,16,128]{4,3,2,1,0:T(8,128)S(1)} %get-tuple-element.67), channel_id=1, source_target_pairs={{0,4},{4,8},{8,12},{12,16},{16,20},{20,24},{24,28},{1,5},{5,9},{9,... | collective-permute-start | bytes 196616 | tf_op jit(solution)/shard_map/ppermute | solution.py:19
  361.1 9.6 %collective-permute-start.32 = (f32[2,4,1,16,128]{4,3,2,1,0:T(8,128)S(1)}, f32[2,4,1,16,128]{4,3,2,1,0:T(8,128)S(1)}, u32[]{:S(2)}, u32[]{:S(2)}) collective-permute-start(f32[2,4,1,16,128]{4,3,2,1,0:T(8,128)S(1)} %get-tuple-element.68), channel_id=1, source_target_pairs={{4,0},{8,4},{12,8},{16,12},{20,16},{24,20},{28,24},{5,1},{9,5},{13... | collective-permute-start | bytes 196616 | tf_op jit(solution)/shard_map/ppermute | solution.py:20
  362.9 29.0 %collective-permute-start.53 = (f32[1,16,128]{1,2,0:T(8,128)}, f32[1,16,128]{1,2,0:T(8,128)}, u32[]{:S(2)}, u32[]{:S(2)}) collective-permute-start(f32[1,16,128]{1,2,0:T(8,128)} %bitcast.29), channel_id=1, source_target_pairs={{0,4},{4,8},{8,12},{12,16},{16,20},{20,24},{24,28},{1,5},{5,9},{9,... | collective-permute-start | bytes 24584 | tf_op jit(solution)/shard_map/ppermute | solution.py:19
  368.4 41.6 %collective-permute-start.56 = (f32[1,16,128]{1,2,0:T(8,128)}, f32[1,16,128]{1,2,0:T(8,128)}, u32[]{:S(2)}, u32[]{:S(2)}) collective-permute-start(f32[1,16,128]{1,2,0:T(8,128)} %bitcast.38), channel_id=1, source_target_pairs={{4,0},{8,4},{12,8},{16,12},{20,16},{24,20},{28,24},{5,1},{9,5},{13... | collective-permute-start | bytes 24584 | tf_op jit(solution)/shard_map/ppermute | solution.py:20
  379.3 15.4 %collective-permute-start.37 = (f32[2,4,1,16,128]{4,3,2,1,0:T(8,128)}, f32[2,4,1,16,128]{4,3,2,1,0:T(8,128)S(1)}, u32[]{:S(2)}, u32[]{:S(2)}) collective-permute-start(f32[2,4,1,16,128]{4,3,2,1,0:T(8,128)} %get-tuple-element.65), channel_id=1, source_target_pairs={{0,4},{4,8},{8,12},{12,16},{16,20},{20,24},{24,28},{1,5},{5,9},{9,... | collective-permute-start | bytes 196616 | tf_op jit(solution)/shard_map/ppermute | solution.py:19
  383.3 11.4 %collective-permute-start.36 = (f32[2,4,1,16,128]{4,3,2,1,0:T(8,128)S(1)}, f32[2,4,1,16,128]{4,3,2,1,0:T(8,128)S(1)}, u32[]{:S(2)}, u32[]{:S(2)}) collective-permute-start(f32[2,4,1,16,128]{4,3,2,1,0:T(8,128)S(1)} %get-tuple-element.66), channel_id=1, source_target_pairs={{4,0},{8,4},{12,8},{16,12},{20,16},{24,20},{28,24},{5,1},{9,5},{13... | collective-permute-start | bytes 196616 | tf_op jit(solution)/shard_map/ppermute | solution.py:20
  385.2 30.5 %collective-permute-start.57 = (f32[1,16,128]{1,2,0:T(8,128)}, f32[1,16,128]{1,2,0:T(8,128)}, u32[]{:S(2)}, u32[]{:S(2)}) collective-permute-start(f32[1,16,128]{1,2,0:T(8,128)} %bitcast.39), channel_id=1, source_target_pairs={{0,4},{4,8},{8,12},{12,16},{16,20},{20,24},{24,28},{1,5},{5,9},{9,... | collective-permute-start | bytes 24584 | tf_op jit(solution)/shard_map/ppermute | solution.py:19
  391.9 56.9 %collective-permute-start.50 = (f32[10,1,128]{2,1,0:T(1,128)}, f32[10,1,128]{2,1,0:T(1,128)}, u32[]{:S(2)}, u32[]{:S(2)}) collective-permute-start(f32[10,1,128]{2,1,0:T(1,128)} %get-tuple-element.97), channel_id=1, source_target_pairs={{1,0},{2,1},{3,2},{5,4},{6,5},{7,6},{9,8},{10,9},{11,10},{13,12},{... | collective-permute-start | bytes 15368 | tf_op jit(solution)/shard_map/ppermute | solution.py:20
  404.4 14.1 %collective-permute-start.41 = (f32[2,4,1,16,128]{4,3,2,1,0:T(8,128)}, f32[2,4,1,16,128]{4,3,2,1,0:T(8,128)S(1)}, u32[]{:S(2)}, u32[]{:S(2)}) collective-permute-start(f32[2,4,1,16,128]{4,3,2,1,0:T(8,128)} %get-tuple-element.63), channel_id=1, source_target_pairs={{0,4},{4,8},{8,12},{12,16},{16,20},{20,24},{24,28},{1,5},{5,9},{9,... | collective-permute-start | bytes 196616 | tf_op jit(solution)/shard_map/ppermute | solution.py:19
  408.0 10.5 %collective-permute-start.40 = (f32[2,4,1,16,128]{4,3,2,1,0:T(8,128)}, f32[2,4,1,16,128]{4,3,2,1,0:T(8,128)S(1)}, u32[]{:S(2)}, u32[]{:S(2)}) collective-permute-start(f32[2,4,1,16,128]{4,3,2,1,0:T(8,128)} %get-tuple-element.64), channel_id=1, source_target_pairs={{4,0},{8,4},{12,8},{16,12},{20,16},{24,20},{28,24},{5,1},{9,5},{13... | collective-permute-start | bytes 196616 | tf_op jit(solution)/shard_map/ppermute | solution.py:20
  410.0 43.0 %collective-permute-start.51 = (f32[10,1,128]{2,1,0:T(1,128)}, f32[10,1,128]{2,1,0:T(1,128)}, u32[]{:S(2)}, u32[]{:S(2)}) collective-permute-start(f32[10,1,128]{2,1,0:T(1,128)} %get-tuple-element.98), channel_id=1, source_target_pairs={{0,1},{1,2},{2,3},{4,5},{5,6},{6,7},{8,9},{9,10},{10,11},{12,13},{... | collective-permute-start | bytes 15368 | tf_op jit(solution)/shard_map/ppermute | solution.py:19
  415.7 37.3 %collective-permute-start.54 = (f32[10,1,128]{2,1,0:T(1,128)}, f32[10,1,128]{2,1,0:T(1,128)}, u32[]{:S(2)}, u32[]{:S(2)}) collective-permute-start(f32[10,1,128]{2,1,0:T(1,128)} %get-tuple-element.99), channel_id=1, source_target_pairs={{1,0},{2,1},{3,2},{5,4},{6,5},{7,6},{9,8},{10,9},{11,10},{13,12},{... | collective-permute-start | bytes 15368 | tf_op jit(solution)/shard_map/ppermute | solution.py:20
  441.8 11.3 %collective-permute-start.55 = (f32[10,1,128]{2,1,0:T(1,128)S(1)}, f32[10,1,128]{2,1,0:T(1,128)S(1)}, u32[]{:S(2)}, u32[]{:S(2)}) collective-permute-start(f32[10,1,128]{2,1,0:T(1,128)S(1)} %copy-done.107), channel_id=1, source_target_pairs={{0,1},{1,2},{2,3},{4,5},{5,6},{6,7},{8,9},{9,10},{10,11},{12,13},{... | collective-permute-start | bytes 15368 | tf_op jit(solution)/shard_map/ppermute | solution.py:19
  (148 other events, 1667.4 us)
Sparse Core Ops, SparseCore 0:
  455.9 48.3 reduce-scatter.3
where the time goes:
time: 516 us; the launch traced here: 513 us
  blocking collectives  198 us (38%)
  starting transfers between devices  168 us (33%)
  waiting for transfers between devices  76.6 us (15%)
  local copies, waits for them, and re-layouts  31.8 us (6%)
  other arithmetic  21.5 us (4%)
  between operations  16.7 us (3%)
    ppermute x30, starting transfers between devices, padded_2(): before = lax.ppermute(last, axis, up)  129 us
    all_gather x3, blocking collectives, local(): lax.all_gather(saved_heat_field[backward_counter], 'obs', axis=2, tiled=T...  57.2 us
    all_gather x3, blocking collectives, local(): lax.all_gather(saved_pore_load[backward_counter], 'obs', axis=2, tiled=True)  50.1 us
    unnamed x2, waiting for transfers between devices  46.6 us
    all_gather x3, blocking collectives, local(): lax.all_gather(saved_dilatation[backward_counter], 'obs', axis=2, tiled=T...  45.5 us
    all_gather x3, blocking collectives, local(): lax.all_gather(saved_conductivity[backward_counter], 'obs', axis=2, tiled...  45.3 us
    ppermute x30, starting transfers between devices, padded_2(): after = lax.ppermute(initial, axis, down)  39 us
    ppermute x30, waiting for transfers between devices, padded_2(): after = lax.ppermute(initial, axis, down)  19 us
  transfers between devices with their start and end apart: 61, of which 19 were waited for; matrix products, arithmetic and copies ran while one was open for 8% of the time, Pallas kernels for 0%

commit v1 on v0

v1 whole, which is shorter than its diff:
```python
import functools

import jax
import jax.numpy as jnp
from jax import lax
from jax.experimental import pallas as pl
from jax.experimental.pallas import tpu as pltpu
from jax.sharding import PartitionSpec as P

MESH = pl.DeviceIdType.MESH
F32 = jnp.float32
ITERS = 4
NX, NY, NZ = 8, 16, 128
NS = 3
NO = 4
NP = 8
LP = NZ // NP
NJ = 8
AP, BP, AT, BT = range(4)
RPC, IP, RTC, KK = range(4)


def role(obs, gx):
    return 2 * (obs // 2) + gx % 2, 2 * (gx // 2) + obs % 2


def regroup(tiles, lane_group):
    turned = [pltpu.roll(t, LP * d, 1) if d else t for d, t in enumerate(tiles)]
    outs = []
    for x in range(NP):
        mixed = turned[(NP - 1 - x) % NP]
        for g in range(NP - 1):
            mixed = jnp.where(lane_group == g, turned[(g - x) % NP], mixed)
        outs.append(pltpu.roll(mixed, NZ - LP * x, 1) if x else mixed)
    return outs


def kernel(
    cost_ref, pore_ref, heat_ref, dil_ref, cond_ref, resid_ref, pos_ref, wgt_ref,
    out_ref, grad_ref,
    saved, pack, gath, raw, meta, meta_in, state, ysend, yrecv, coef, crep, prep_pore, ypore, ycol, prow, pcol,
    right, gacc, gpack, gred, outst,
    load_sem, gsend, grecv, ssend, srecv, msem, hsend, hrecv, psend, precv, osend, orecv, rsend, rrecv,
):
    obs, gx, gy = lax.axis_index("obs"), lax.axis_index("gx"), lax.axis_index("gy")
    lobs, lgx = role(obs, gx)
    stays = jnp.logical_and(lobs == obs, lgx == gx)
    moves = jnp.logical_not(stays)
    zh, yy = obs // 2, gx // 2
    ngx, ngy = lax.axis_size("gx"), lax.axis_size("gy")

    lane = lax.broadcasted_iota(jnp.int32, (8, NZ), 1)
    sub = lax.broadcasted_iota(jnp.int32, (8, NZ), 0)
    lane_group = lane // LP
    first_lane, last_lane = lane == 0, lane == NZ - 1
    even = sub % 2 == 0

    exists = (lgx > 0, lgx < ngx - 1, gy > 0, gy < ngy - 1)
    xm = role(lobs, jnp.maximum(lgx - 1, 0))
    xp = role(lobs, jnp.minimum(lgx + 1, ngx - 1))
    near = (
        (xm[0], xm[1], gy),
        (xp[0], xp[1], gy),
        (obs, gx, jnp.maximum(gy - 1, 0)),
        (obs, gx, jnp.minimum(gy + 1, ngy - 1)),
    )
    partner = (lobs, lgx, gy)

    fields = (pore_ref, heat_ref, dil_ref, cond_ref)

    def load(n, f):
        return pltpu.make_async_copy(fields[f].at[n], saved.at[n, f], load_sem.at[n, f])

    for n in range(NS - 1, -1, -1):
        for f in range(4):
            load(n, f).start()

    zero = jnp.zeros((8, NZ), F32)
    for slot in range(2):
        for row in (0, NX + 1):
            state[slot, row] = jnp.zeros((2 * NJ * 8, NZ), F32)
    yrecv[...] = jnp.zeros(yrecv.shape, F32)
    prow[...] = jnp.zeros(prow.shape, F32)
    pcol[...] = jnp.zeros(pcol.shape, F32)

    barrier = pltpu.get_barrier_semaphore()
    for zz in range(4):
        for core in range(2):
            for low in range(2):
                there = (2 * zz + core, 2 * yy + low, gy)

                @pl.when(jnp.logical_or(there[0] != obs, there[1] != gx))
                def _(there=there):
                    pl.semaphore_signal(barrier, inc=1, device_id=there, device_id_type=MESH)

    for k in range(4):

        @pl.when(exists[k])
        def _(k=k):
            pl.semaphore_signal(barrier, inc=1, device_id=near[k], device_id_type=MESH)

    count = 15
    for k in range(4):
        count = count + exists[k].astype(jnp.int32)
    pl.semaphore_wait(barrier, count)

    srow = sub // 2
    for n in range(NS):
        tile = zero
        for o in range(NO):
            tile = jnp.where(srow == o, jnp.broadcast_to(resid_ref[n, o : o + 1, :], (8, NZ)), tile)
        meta[n] = tile
    pos = jnp.zeros((8, NZ), jnp.int32)
    wgt = jnp.zeros((8, NZ), jnp.int32)
    for o in range(NO):
        pos = jnp.where(srow == o, pos_ref[o], pos)
        wgt = jnp.where(srow == o, wgt_ref[o], wgt)
    meta[3] = pos.astype(F32)
    meta[4] = wgt.astype(F32)

    def gather_copy(n, target):
        return pltpu.make_async_remote_copy(
            src_ref=pack.at[n],
            dst_ref=gath.at[n, obs],
            send_sem=gsend.at[n, target],
            recv_sem=grecv.at[n, obs],
            device_id=(2 * (target // 2) + gx % 2, 2 * yy + target % 2, gy),
            device_id_type=MESH,
        )

    def is_me(target):
        return jnp.logical_and(stays, lobs == target)

    def send_saved(n):
        for f in range(4):
            load(n, f).wait()
        for f in range(4):
            for h in range(2):
                packed = saved_tile(n, f, 0, h)
                for x in range(1, NX):
                    packed = jnp.where(
                        lane_group == x, pltpu.roll(saved_tile(n, f, x, h), LP * x, 1), packed
                    )
                pack[n, pl.ds((f * 2 + h) * 8, 8), :] = packed

                @pl.when(stays)
                def _(packed=packed, f=f, h=h):
                    gath[n, obs, pl.ds((f * 2 + h) * 8, 8), :] = packed

        for target in range(NP):

            @pl.when(jnp.logical_not(is_me(target)))
            def _(target=target):
                gather_copy(n, target).start()

    def saved_tile(n, f, x, h):
        piece = saved[n, f, x, pl.ds(h * 8, 8), :]
        return jnp.concatenate([piece, jnp.zeros((8, NZ - LP), F32)], axis=1)

    def swap_in(k):
        return pltpu.make_async_remote_copy(
            src_ref=cost_ref.at[k // NO, k % NO],
            dst_ref=raw.at[:, pl.ds(k * NY, NY), :],
            send_sem=ssend.at[k],
            recv_sem=srecv.at[k],
            device_id=partner,
            device_id_type=MESH,
        )

    def keep_in(k):
        return pltpu.make_async_copy(
            cost_ref.at[k // NO, k % NO], raw.at[:, pl.ds(k * NY, NY), :], srecv.at[k]
        )

    def send_meta():
        return pltpu.make_async_remote_copy(
            src_ref=meta, dst_ref=meta_in, send_sem=msem.at[0], recv_sem=msem.at[1], device_id=partner, device_id_type=MESH
        )

    send_saved(NS - 1)

    @pl.when(moves)
    def _():
        send_meta().start()
        for k in range(2 * NO):
            swap_in(k).start()

    @pl.when(stays)
    def _():
        for k in range(2 * NO):
            keep_in(k).start()
        meta_in[...] = meta[...]

    for n in range(NS - 2, -1, -1):
        send_saved(n)

    @pl.when(moves)
    def _():
        send_meta().wait()
        for k in range(2 * NO):
            swap_in(k).wait()

    @pl.when(stays)
    def _():
        for k in range(2 * NO):
            keep_in(k).wait()

    def halo(slot, k):
        if k == 0:
            src, dst = state.at[slot, 1], state.at[slot, NX + 1]
        elif k == 1:
            src, dst = state.at[slot, NX], state.at[slot, 0]
        elif k == 2:
            src, dst = ysend.at[slot, 0], yrecv.at[slot, 1]
        else:
            src, dst = ysend.at[slot, 1], yrecv.at[slot, 0]
        return pltpu.make_async_remote_copy(
            src_ref=src,
            dst_ref=dst,
            send_sem=hsend.at[slot, k],
            recv_sem=hrecv.at[slot, k ^ 1],
            device_id=near[k],
            device_id_type=MESH,
        )

    def start_halos(slot):
        for k in range(4):

            @pl.when(exists[k])
            def _(k=k):
                halo(slot, k).start()

    def wait_halos(slot):
        for k in range(4):

            @pl.when(exists[k])
            def _(k=k):
                halo(slot, k ^ 1).wait_recv()
                halo(slot, k).wait_send()

    def y_message(slot, x, p, t):
        ysend[slot, 0, pl.ds(x * 8, 8), :] = jnp.where(even, p[0], pltpu.roll(t[0], 1, 0))
        ysend[slot, 1, pl.ds(x * 8, 8), :] = jnp.where(even, pltpu.roll(p[1], 7, 0), t[1])

    def first_row(x, _):
        ends = []
        for f in range(2):
            tiles = [raw[x, pl.ds(f * 64 + j, 8, stride=8), :] for j in range(NJ)]
            for j in range(NJ):
                state[0, x + 1, pl.ds((f * NJ + j) * 8, 8), :] = tiles[j]
            ends.append((tiles[0], tiles[-1]))
        y_message(0, x, *ends)
        return 0

    lax.fori_loop(0, NX, first_row, 0)
    start_halos(0)

    def around(tiles, up, down, before, after):
        sums = []
        for j in range(NJ):
            here = tiles[j]
            total = up[j] + down[j]
            total = total + (tiles[j - 1] if j else before) + (tiles[j + 1] if j < NJ - 1 else after)
            deep = jnp.where(first_lane, 0.0, pltpu.roll(here, 1, 1))
            shallow = jnp.where(last_lane, 0.0, pltpu.roll(here, NZ - 1, 1))
            sums.append(total + deep + shallow)
        return sums

    def relax_row(slot, x, last):
        tiles = [[state[slot, x + 1, pl.ds((f * NJ + j) * 8, 8), :] for j in range(NJ)] for f in range(2)]
        up = [[state[slot, x, pl.ds((f * NJ + j) * 8, 8), :] for j in range(NJ)] for f in range(2)]
        down = [[state[slot, x + 2, pl.ds((f * NJ + j) * 8, 8), :] for j in range(NJ)] for f in range(2)]
        low = yrecv[slot, 0, pl.ds(x * 8, 8), :]
        high = yrecv[slot, 1, pl.ds(x * 8, 8), :]
        lows = (low, pltpu.roll(low, 7, 0))
        highs = (pltpu.roll(high, 1, 0), high)
        sums = []
        for f in range(2):
            before = jnp.where(even, lows[f], pltpu.roll(tiles[f][-1], 1, 0))
            after = jnp.where(even, pltpu.roll(tiles[f][0], 7, 0), highs[f])
            sums.append(around(tiles[f], up[f], down[f], before, after))
        ends = [[], []]
        for j in range(NJ):
            at = pl.ds(j * 8, 8)
            new_p = (
                right[x, at, :] + coef[AP, x, at, :] * sums[0][j] + coef[BP, x, at, :] * tiles[1][j]
            )
            new_t = (
                right[x, pl.ds((NJ + j) * 8, 8), :]
                + coef[AT, x, at, :] * sums[1][j]
                + coef[BT, x, at, :] * new_p
            )
            state[1 - slot, x + 1, at, :] = new_p
            state[1 - slot, x + 1, pl.ds((NJ + j) * 8, 8), :] = new_t
            if j in (0, NJ - 1):
                ends[0].append(new_p)
                ends[1].append(new_t)
        y_message(1 - slot, x, *ends)

    base_cell = (lgx * NX) * (ngy * NY) + gy * NY

    def pore_halo(n, k):
        if k == 0:
            src, dst = ypore.at[n, pl.ds(0, NY)], prow.at[n, 1]
        elif k == 1:
            src, dst = ypore.at[n, pl.ds((NX - 1) * NY, NY)], prow.at[n, 0]
        elif k == 2:
            src, dst = ycol.at[n, 0], pcol.at[n, 1]
        else:
            src, dst = ycol.at[n, 1], pcol.at[n, 0]
        return pltpu.make_async_remote_copy(
            src_ref=src,
            dst_ref=dst,
            send_sem=psend.at[n, k],
            recv_sem=precv.at[n, k ^ 1],
            device_id=near[k],
            device_id_type=MESH,
        )

    def repeat(ref, lead, h, value):
        for o in range(NO):
            ref[(*lead, pl.ds(o * NY + h * 8, 8), slice(None))] = value

    def prepare(n):
        for d in range(NP):

            @pl.when(jnp.logical_not(jnp.logical_and(stays, obs == d)))
            def _(d=d):
                pltpu.make_async_remote_copy(
                    src_ref=pack.at[n],
                    dst_ref=gath.at[n, d],
                    send_sem=gsend.at[n, d],
                    recv_sem=grecv.at[n, d],
                    device_id=partner,
                    device_id_type=MESH,
                ).wait_recv()

        for h in range(2):
            whole = [
                regroup([gath[n, d, pl.ds((f * 2 + h) * 8, 8), :] for d in range(NP)], lane_group) for f in range(4)
            ]
            for x in range(NX):
                pore, heat, dil, perm = (whole[f][x] for f in range(4))
                store_p = jnp.exp(dil)
                store_t = jnp.exp(0.5 * heat)
                coupling = 0.2 * jnp.tanh(pore)
                inv_p = 1.0 / (store_p + 6.0 * perm)
                inv_t = 1.0 / (store_t + 12.0)
                rows = {
                    0: perm * inv_p,
                    1: coupling * inv_p,
                    2: 2.0 * inv_t,
                    3: coupling * inv_t,
                    4: store_p * inv_p,
                    5: inv_p,
                    6: store_t * inv_t,
                    7: perm,
                }
                for c, value in rows.items():
                    repeat(crep, (c, x), h, value)
                repeat(prep_pore, (x + 1,), h, pore)
                ypore[n, pl.ds(x * NY + h * 8, 8), :] = pore
        for side, y in ((0, 0), (1, NY - 1)):
            ycol[n, side] = ypore[n, pl.ds(y, NX, stride=NY), :]
        for k in range(4):

            @pl.when(exists[k])
            def _(k=k):
                pore_halo(n, k).start()

        source = meta_in[n]
        cell = meta_in[3] - (8 * (sub % 2) + base_cell).astype(F32)

        def spread(x, _):
            for j in range(NJ):
                at = pl.ds(j * 8, 8)
                for c in range(4):
                    coef[c, x, at, :] = crep[c, x, pl.ds(j, 8, stride=8), :]
                mine = cell == (x * (ngy * NY) + j).astype(F32)
                term = jnp.where(mine, source, 0.0)
                right[x, at, :] = (
                    crep[4, x, pl.ds(j, 8, stride=8), :] * state[0, x + 1, at, :]
                    + crep[5, x, pl.ds(j, 8, stride=8), :] * term
                )
                right[x, pl.ds((NJ + j) * 8, 8), :] = (
                    crep[6, x, pl.ds(j, 8, stride=8), :] * state[0, x + 1, pl.ds((NJ + j) * 8, 8), :]
                )
            return 0

        lax.fori_loop(0, NX, spread, 0)

    def add_gradient(n):
        for k in range(4):

            @pl.when(exists[k])
            def _(k=k):
                pore_halo(n, k ^ 1).wait_recv()
                pore_halo(n, k).wait_send()

        for side, row in ((0, 0), (1, NX + 1)):
            for h in range(2):
                repeat(prep_pore, (row,), h, prow[n, side, pl.ds(h * 8, 8), :])
        weight = meta_in[4]

        def row(x, _):
            tiles, up, down = (
                [prep_pore[x + dx, pl.ds(j, 8, stride=8), :] for j in range(NJ)] for dx in (1, 0, 2)
            )
            low = jnp.broadcast_to(pcol[n, 0, pl.ds(x, 1), :], (8, NZ))
            high = jnp.broadcast_to(pcol[n, 1, pl.ds(x, 1), :], (8, NZ))
            before = jnp.where(even, low, pltpu.roll(tiles[-1], 1, 0))
            after = jnp.where(even, pltpu.roll(tiles[0], 7, 0), high)
            sums = around(tiles, up, down, before, after)
            for j in range(NJ):
                at = pl.ds(j * 8, 8)
                laplace = sums[j] - 6.0 * tiles[j]
                gacc[x, at, :] += (
                    crep[7, x, pl.ds(j, 8, stride=8), :] * laplace * (weight * state[0, x + 1, at, :])
                )
            return 0

        lax.fori_loop(0, NX, row, 0)

    def swap_out(k):
        return pltpu.make_async_remote_copy(
            src_ref=outst.at[:, pl.ds(k * NY, NY), :],
            dst_ref=out_ref.at[k // NO, k % NO],
            send_sem=osend.at[k],
            recv_sem=orecv.at[k],
            device_id=partner,
            device_id_type=MESH,
        )

    def keep_out(k):
        return pltpu.make_async_copy(
            outst.at[:, pl.ds(k * NY, NY), :], out_ref.at[k // NO, k % NO], orecv.at[k]
        )

    def finish():
        def row(x, _):
            for f in range(2):
                for o in range(NO):
                    for h in range(2):
                        outst[x, pl.ds((f * NO + o) * NY + h * 8, 8), :] = state[
                            0, x + 1, pl.ds(f * 64 + 2 * o + h, 8, stride=8), :
                        ]
            return 0

        lax.fori_loop(0, NX, row, 0)

        @pl.when(moves)
        def _():
            for k in range(2 * NO):
                swap_out(k).start()

        @pl.when(stays)
        def _():
            for k in range(2 * NO):
                keep_out(k).start()

    gacc[...] = jnp.zeros(gacc.shape, F32)

    def step(i, _):
        n = NS - 1 - i
        prepare(n)
        for sweep in range(ITERS):
            slot = sweep % 2
            wait_halos(slot)

            def row(x, _, slot=slot):
                relax_row(slot, x, False)
                return 0

            lax.fori_loop(0, NX, row, 0, unroll=2)
            if sweep < ITERS - 1:
                start_halos(1 - slot)

        @pl.when(n > 0)
        def _():
            start_halos(0)

        @pl.when(n == 0)
        def _():
            finish()

        add_gradient(n)
        return 0

    lax.fori_loop(0, NS, step, 0)

    for h in range(2):
        whole = []
        for x in range(NX):
            total = gacc[x, pl.ds(h, 8, stride=8), :]
            for o in range(1, NO):
                total = total + gacc[x, pl.ds(2 * o + h, 8, stride=8), :]
            whole.append(total)
        for d, tile in enumerate(regroup(whole, lane_group)):
            gpack[d, pl.ds(h * 8, 8), :] = tile

            @pl.when(jnp.logical_and(stays, obs == d))
            def _(tile=tile, h=h):
                gred[lobs, pl.ds(h * 8, 8), :] = tile

    def reduce_copy(d):
        return pltpu.make_async_remote_copy(
            src_ref=gpack.at[d],
            dst_ref=gred.at[lobs],
            send_sem=rsend.at[d],
            recv_sem=rrecv.at[lobs],
            device_id=(d, lgx, gy),
            device_id_type=MESH,
        )

    for d in range(NP):

        @pl.when(jnp.logical_not(jnp.logical_and(stays, obs == d)))
        def _(d=d):
            reduce_copy(d).start()

    for d in range(NP):

        @pl.when(jnp.logical_not(is_me(d)))
        def _(d=d):
            pltpu.make_async_remote_copy(
                src_ref=gpack.at[d],
                dst_ref=gred.at[d],
                send_sem=rsend.at[d],
                recv_sem=rrecv.at[d],
                device_id=partner,
                device_id_type=MESH,
            ).wait_recv()

    for h in range(2):
        total = gred[0, pl.ds(h * 8, 8), :]
        for d in range(1, NP):
            total = total + gred[d, pl.ds(h * 8, 8), :]
        for x in range(NX):
            turned = pltpu.roll(total, NZ - LP * x, 1) if x else total
            grad_ref[x, pl.ds(h * 8, 8), :] = turned[:, :LP]

    for d in range(NP):

        @pl.when(jnp.logical_not(jnp.logical_and(stays, obs == d)))
        def _(d=d):
            reduce_copy(d).wait_send()

    for n in range(NS):
        for target in range(NP):

            @pl.when(jnp.logical_not(is_me(target)))
            def _(n=n, target=target):
                gather_copy(n, target).wait_send()

    @pl.when(moves)
    def _():
        for k in range(2 * NO):
            swap_out(k).wait()

    @pl.when(stays)
    def _():
        for k in range(2 * NO):
            keep_out(k).wait()


def local(*args):
    hbm = pl.BlockSpec(memory_space=pl.ANY)
    vmem = pl.BlockSpec(memory_space=pltpu.VMEM)
    smem = pl.BlockSpec(memory_space=pltpu.SMEM)
    dma = pltpu.SemaphoreType.DMA
    rows = 2 * NJ * 8
    return pl.pallas_call(
        kernel,
        out_shape=(
            jax.ShapeDtypeStruct((2, NO, NX, NY, NZ), F32),
            jax.ShapeDtypeStruct((NX, NY, LP), F32),
        ),
        in_specs=[hbm, hbm, hbm, hbm, hbm, vmem, smem, smem],
        out_specs=(hbm, vmem),
        scratch_shapes=[
            pltpu.VMEM((NS, 4, NX, NY, LP), F32),
            pltpu.VMEM((NS, 64, NZ), F32),
            pltpu.VMEM((NS, NP, 64, NZ), F32),
            pltpu.VMEM((NX, rows, NZ), F32),
            pltpu.VMEM((5, 8, NZ), F32),
            pltpu.VMEM((5, 8, NZ), F32),
            pltpu.VMEM((2, NX + 2, rows, NZ), F32),
            pltpu.VMEM((2, 2, NX * 8, NZ), F32),
            pltpu.VMEM((2, 2, NX * 8, NZ), F32),
            pltpu.VMEM((4, NX, 64, NZ), F32),
            pltpu.VMEM((8, NX, 64, NZ), F32),
            pltpu.VMEM((NX + 2, 64, NZ), F32),
            pltpu.VMEM((NS, NX * NY, NZ), F32),
            pltpu.VMEM((NS, 2, 8, NZ), F32),
            pltpu.VMEM((NS, 2, NY, NZ), F32),
            pltpu.VMEM((NS, 2, 8, NZ), F32),
            pltpu.VMEM((NX, rows, NZ), F32),
            pltpu.VMEM((NX, 64, NZ), F32),
            pltpu.VMEM((NP, NY, NZ), F32),
            pltpu.VMEM((NP, NY, NZ), F32),
            pltpu.VMEM((NX, rows, NZ), F32),
            dma((NS, 4)),
            dma((NS, NP)),
            dma((NS, NP)),
            dma((2 * NO,)),
            dma((2 * NO,)),
            dma((2,)),
            dma((2, 4)),
            dma((2, 4)),
            dma((NS, 4)),
            dma((NS, 4)),
            dma((2 * NO,)),
            dma((2 * NO,)),
            dma((NP,)),
            dma((NP,)),
        ],
        compiler_params=pltpu.CompilerParams(
            collective_id=0, has_side_effects=True, vmem_limit_bytes=48 * 1024 * 1024
        ),
    )(*args)


def solution(mesh):
    return jax.shard_map(
        local,
        mesh=mesh,
        in_specs=(
            P(None, "obs", "gx", "gy", None),
            P(None, "gx", "gy", "obs"),
            P(None, "gx", "gy", "obs"),
            P(None, "gx", "gy", "obs"),
            P(None, "gx", "gy", "obs"),
            P(None, "obs", None),
            P("obs"),
            P("obs"),
        ),
        out_specs=(P(None, "obs", "gx", "gy", None), P("gx", "gy", "obs")),
        check_vma=False,
    )
```

time: 516 us -> 95.8 us (0.19)
  blocking collectives: 198 us -> 0 us
  starting transfers between devices: 168 us -> 0 us
  Pallas kernels: 0 us -> 86.7 us
  waiting for transfers between devices: 76.6 us -> 0 us
  local copies, waits for them, and re-layouts: 31.8 us -> 8.17 us
  other arithmetic: 21.5 us -> 0 us
  between operations: 16.7 us -> 0.66 us
    all_gather x12 -> x0, blocking collectives: 198 us -> none  [the longest x3 57.2 us: local(): lax.all_gather(saved_heat_field[backward_counter], 'obs', axis=2, tiled=T...]
    ppermute x60 -> x0, starting transfers between devices: 168 us -> none  [the longest x30 129 us: padded_2(): before = lax.ppermute(last, axis, up)]
    pallas_call x0 -> x1, Pallas kernels: none -> 86.7 us  [local(): pl.pallas_call(kernel, out_shape=(jax.ShapeDtypeStruct((2, NO, NX, NY, NZ...]
    unnamed x2 -> x0, waiting for transfers between devices: 46.6 us -> none
    ppermute x60 -> x0, waiting for transfers between devices: 30 us -> none  [the longest x30 19 us: padded_2(): after = lax.ppermute(initial, axis, down)]
    add x21 -> x0, other arithmetic: 8.82 us -> none  [the longest x12 5.26 us: neighbour_sum(): return summed + deeper[..., 2:] + deeper[..., :-2]]
    ppermute x6 -> x0, local copies, waits for them, and re-layouts: 7.79 us -> none  [the longest x3 3.9 us: padded_2(): before = lax.ppermute(last, axis, up)]
    all_gather x12 -> x0, local copies, waits for them, and re-layouts: 5.52 us -> none  [the longest x3 2.21 us: local(): lax.all_gather(saved_heat_field[backward_counter], 'obs', axis=2, tiled=T...]
  transfers between devices with their start and end apart: 61 -> 0, of which waited for: 19 -> 0; matrix products, arithmetic and copies ran while one was open for 8% -> 0% of each run, Pallas kernels for 0% -> 0%
where the time goes in v1:
time: 95.8 us; the launch traced here: 95.5 us
  Pallas kernels  86.7 us (91%)
  local copies, waits for them, and re-layouts  8.17 us (9%)
    pallas_call x1, Pallas kernels, local(): pl.pallas_call(kernel, out_shape=(jax.ShapeDtypeStruct((2, NO, NX, NY, NZ...  86.7 us
    unnamed x18, local copies, waits for them, and re-layouts  8.17 us

profile of v1, /device:TPU:1, one launch (start us, length us, event | category | flops | bytes accessed | tf_op | source)
XLA Modules:
  0.0 95.5 jit_solution(4488813063486256590)
XLA Ops:
  0.6 0.0 copy-start
  0.6 1.0 %copy-done = f32[2,4,8,16,128]{4,3,2,1,0:T(8,128)S(1)} copy-done((f32[2,4,8,16,128]{4,3,2,1,0:T(8,128)S(1)}, f32[2,4,8,16,128]{4,3,2,1,0:T(8,128)}, u32[]{:S(2)}) %copy-start) | copy-done | bytes 524312
  1.7 0.0 copy-start.1
  1.7 0.9 copy-done.1
  2.6 0.0 copy-start.2
  2.6 0.9 copy-done.2
  3.5 0.0 copy-start.3
  3.5 0.9 copy-done.3
  4.5 0.0 copy-start.4
  4.5 0.9 copy-done.4
  5.4 0.0 copy-start.5
  5.4 0.7 copy-done.5
  6.1 0.0 copy-start.6
  6.1 0.7 copy-done.6
  6.7 0.0 copy-start.7
  6.7 0.7 copy-done.7
  7.4 86.7 %shard_map.95 = (f32[2,4,8,16,128]{4,3,2,1,0:T(8,128)S(1)}, f32[8,16,16]{2,1,0:T(8,128)S(1)}) custom-call(f32[2,4,8,16,128]{4,3,2,1,0:T(8,128)S(1)} %copy-done, f32[3,8,16,16]{3,2,1,0:T(8,128)S(1)} %copy-done.1, f32[3,8,16,16]{3,2,1,0:T(8,128)S(1)} %copy-done.2, f32[3,8,16,16]{3,2,1,0:T(8,128)S(1)} %copy-done.3, f32[3,8,16,16]{3,2,1,0:T(8,128)S(1)} %copy-done.4, ...), custom_call_target="tpu_custom_call" | custom-call | tf_op jit(solution)/shard_map/pallas_call | solution.py:572
  94.1 0.8 copy.12
  94.9 0.6 copy.13
Async XLA Ops:
  0.6 1.0 %copy-start = (f32[2,4,8,16,128]{4,3,2,1,0:T(8,128)S(1)}, f32[2,4,8,16,128]{4,3,2,1,0:T(8,128)}, u32[]{:S(2)}) copy-start(f32[2,4,8,16,128]{4,3,2,1,0:T(8,128)} %cost_ref.1) | copy-start | bytes 1572868
  1.7 0.9 copy-start.1
  2.6 0.9 copy-start.2
  3.5 0.9 copy-start.3
  4.5 0.9 copy-start.4
  5.4 0.7 copy-start.5
  6.1 0.7 copy-start.6
  6.7 0.7 copy-start.7

commit v2 on v1

--- a/solution.py
+++ b/solution.py
@@ -10,14 +10,20 @@
 MESH = pl.DeviceIdType.MESH
 F32 = jnp.float32
 ITERS = 4
+UNROLL = 2
 NX, NY, NZ = 8, 16, 128
 NS = 3
 NO = 4
 NP = 8
 LP = NZ // NP
-NJ = 8
-AP, BP, AT, BT = range(4)
-RPC, IP, RTC, KK = range(4)
+SO = 2
+ST = NO // SO
+NQ = 8 // SO
+NJ = NY // NQ
+NG = NQ // 2
+XG = NX // NG
+ROWS = 2 * NJ * 8
+AP, BP, AT, BT, RPC, IP, RTC, KK = range(8)
 
 
 def role(obs, gx):
@@ -39,7 +45,7 @@
     cost_ref, pore_ref, heat_ref, dil_ref, cond_ref, resid_ref, pos_ref, wgt_ref,
     out_ref, grad_ref,
     saved, pack, gath, raw, meta, meta_in, state, ysend, yrecv, coef, crep, prep_pore, ypore, ycol, prow, pcol,
-    right, gacc, gpack, gred, outst,
+    right, gacc, gsum, gpack, gred, outst,
     load_sem, gsend, grecv, ssend, srecv, msem, hsend, hrecv, psend, precv, osend, orecv, rsend, rrecv,
 ):
     obs, gx, gy = lax.axis_index("obs"), lax.axis_index("gx"), lax.axis_index("gy")
@@ -53,7 +59,6 @@
     sub = lax.broadcasted_iota(jnp.int32, (8, NZ), 0)
     lane_group = lane // LP
     first_lane, last_lane = lane == 0, lane == NZ - 1
-    even = sub % 2 == 0
 
     exists = (lgx > 0, lgx < ngx - 1, gy > 0, gy < ngy - 1)
     xm = role(lobs, jnp.maximum(lgx - 1, 0))
@@ -76,9 +81,10 @@
             load(n, f).start()
 
     zero = jnp.zeros((8, NZ), F32)
-    for slot in range(2):
-        for row in (0, NX + 1):
-            state[slot, row] = jnp.zeros((2 * NJ * 8, NZ), F32)
+    for st in range(ST):
+        for slot in range(2):
+            for row in (0, NX + 1):
+                state[st, slot, row] = jnp.zeros((ROWS, NZ), F32)
     yrecv[...] = jnp.zeros(yrecv.shape, F32)
     prow[...] = jnp.zeros(prow.shape, F32)
     pcol[...] = jnp.zeros(pcol.shape, F32)
@@ -104,19 +110,22 @@
         count = count + exists[k].astype(jnp.int32)
     pl.semaphore_wait(barrier, count)
 
-    srow = sub // 2
-    for n in range(NS):
-        tile = zero
-        for o in range(NO):
-            tile = jnp.where(srow == o, jnp.broadcast_to(resid_ref[n, o : o + 1, :], (8, NZ)), tile)
-        meta[n] = tile
-    pos = jnp.zeros((8, NZ), jnp.int32)
-    wgt = jnp.zeros((8, NZ), jnp.int32)
-    for o in range(NO):
-        pos = jnp.where(srow == o, pos_ref[o], pos)
-        wgt = jnp.where(srow == o, wgt_ref[o], wgt)
-    meta[3] = pos.astype(F32)
-    meta[4] = wgt.astype(F32)
+    srow = sub // NQ
+    squarter = sub % NQ
+    for st in range(ST):
+        for n in range(NS):
+            tile = zero
+            for o in range(SO):
+                k = st * SO + o
+                tile = jnp.where(srow == o, jnp.broadcast_to(resid_ref[n, k : k + 1, :], (8, NZ)), tile)
+            meta[st, n] = tile
+        pos = jnp.zeros((8, NZ), jnp.int32)
+        wgt = jnp.zeros((8, NZ), jnp.int32)
+        for o in range(SO):
+            pos = jnp.where(srow == o, pos_ref[st * SO + o], pos)
+            wgt = jnp.where(srow == o, wgt_ref[st * SO + o], wgt)
+        meta[st, 3] = pos.astype(F32)
+        meta[st, 4] = wgt.astype(F32)
 
     def gather_copy(n, target):
         return pltpu.make_async_remote_copy(
@@ -177,83 +186,94 @@
             src_ref=meta, dst_ref=meta_in, send_sem=msem.at[0], recv_sem=msem.at[1], device_id=partner, device_id_type=MESH
         )
 
+    def streams_obs(st):
+        return [f * NO + st * SO + o for f in range(2) for o in range(SO)]
+
     send_saved(NS - 1)
 
     @pl.when(moves)
     def _():
         send_meta().start()
-        for k in range(2 * NO):
-            swap_in(k).start()
+        for st in range(ST):
+            for k in streams_obs(st):
+                swap_in(k).start()
 
     @pl.when(stays)
     def _():
-        for k in range(2 * NO):
-            keep_in(k).start()
+        for st in range(ST):
+            for k in streams_obs(st):
+                keep_in(k).start()
         meta_in[...] = meta[...]
 
-    for n in range(NS - 2, -1, -1):
-        send_saved(n)
-
-    @pl.when(moves)
-    def _():
-        send_meta().wait()
-        for k in range(2 * NO):
-            swap_in(k).wait()
-
-    @pl.when(stays)
-    def _():
-        for k in range(2 * NO):
-            keep_in(k).wait()
-
-    def halo(slot, k):
+    def halo(st, slot, k):
         if k == 0:
-            src, dst = state.at[slot, 1], state.at[slot, NX + 1]
+            src, dst = state.at[st, slot, 1], state.at[st, slot, NX + 1]
         elif k == 1:
-            src, dst = state.at[slot, NX], state.at[slot, 0]
+            src, dst = state.at[st, slot, NX], state.at[st, slot, 0]
         elif k == 2:
-            src, dst = ysend.at[slot, 0], yrecv.at[slot, 1]
+            src, dst = ysend.at[st, slot, 0], yrecv.at[st, slot, 1]
         else:
-            src, dst = ysend.at[slot, 1], yrecv.at[slot, 0]
+            src, dst = ysend.at[st, slot, 1], yrecv.at[st, slot, 0]
         return pltpu.make_async_remote_copy(
             src_ref=src,
             dst_ref=dst,
-            send_sem=hsend.at[slot, k],
-            recv_sem=hrecv.at[slot, k ^ 1],
+            send_sem=hsend.at[st, slot, k],
+            recv_sem=hrecv.at[st, slot, k ^ 1],
             device_id=near[k],
             device_id_type=MESH,
         )
 
-    def start_halos(slot):
+    def start_halos(st, slot):
         for k in range(4):
 
             @pl.when(exists[k])
             def _(k=k):
-                halo(slot, k).start()
-
-    def wait_halos(slot):
+                halo(st, slot, k).start()
+
+    def wait_halos(st, slot):
         for k in range(4):
 
             @pl.when(exists[k])
             def _(k=k):
-                halo(slot, k ^ 1).wait_recv()
-                halo(slot, k).wait_send()
-
-    def y_message(slot, x, p, t):
-        ysend[slot, 0, pl.ds(x * 8, 8), :] = jnp.where(even, p[0], pltpu.roll(t[0], 1, 0))
-        ysend[slot, 1, pl.ds(x * 8, 8), :] = jnp.where(even, pltpu.roll(p[1], 7, 0), t[1])
-
-    def first_row(x, _):
-        ends = []
-        for f in range(2):
-            tiles = [raw[x, pl.ds(f * 64 + j, 8, stride=8), :] for j in range(NJ)]
-            for j in range(NJ):
-                state[0, x + 1, pl.ds((f * NJ + j) * 8, 8), :] = tiles[j]
-            ends.append((tiles[0], tiles[-1]))
-        y_message(0, x, *ends)
-        return 0
-
-    lax.fori_loop(0, NX, first_row, 0)
-    start_halos(0)
+                halo(st, slot, k ^ 1).wait_recv()
+                halo(st, slot, k).wait_send()
+
+    def y_message(st, slot, xg, firsts, lasts):
+        low, high = firsts[0], pltpu.roll(lasts[0], (9 - NQ) % 8, 0)
+        for i in range(1, NQ):
+            low = jnp.where(squarter == i, pltpu.roll(firsts[i], i, 0), low)
+            turned = lasts[i] if i == NQ - 1 else pltpu.roll(lasts[i], (9 + i - NQ) % 8, 0)
+            high = jnp.where(squarter == i, turned, high)
+        ysend[st, slot, 0, pl.ds(xg * 8, 8), :] = low
+        ysend[st, slot, 1, pl.ds(xg * 8, 8), :] = high
+
+    def set_up(st):
+        @pl.when(moves)
+        def _():
+            for k in streams_obs(st):
+                swap_in(k).wait()
+
+        @pl.when(stays)
+        def _():
+            for k in streams_obs(st):
+                keep_in(k).wait()
+
+        def first_rows(xg, _):
+            firsts, lasts = [], []
+            for g in range(NG):
+                x = xg + g * XG
+                for f in range(2):
+                    start = (f * NO + st * SO) * NY
+                    tiles = [raw[x, pl.ds(start + j, 8, stride=NJ), :] for j in range(NJ)]
+                    for j in range(NJ):
+                        state[st, 0, x + 1, pl.ds((f * NJ + j) * 8, 8), :] = tiles[j]
+                    firsts.append(tiles[0])
+                    lasts.append(tiles[-1])
+            y_message(st, 0, xg, firsts, lasts)
+            return 0
+
+        lax.fori_loop(0, XG, first_rows, 0)
+        start_halos(st, 0)
 
     def around(tiles, up, down, before, after):
         sums = []
@@ -266,36 +286,41 @@
             sums.append(total + deep + shallow)
         return sums
 
-    def relax_row(slot, x, last):
-        tiles = [[state[slot, x + 1, pl.ds((f * NJ + j) * 8, 8), :] for j in range(NJ)] for f in range(2)]
-        up = [[state[slot, x, pl.ds((f * NJ + j) * 8, 8), :] for j in range(NJ)] for f in range(2)]
-        down = [[state[slot, x + 2, pl.ds((f * NJ + j) * 8, 8), :] for j in range(NJ)] for f in range(2)]
-        low = yrecv[slot, 0, pl.ds(x * 8, 8), :]
-        high = yrecv[slot, 1, pl.ds(x * 8, 8), :]
-        lows = (low, pltpu.roll(low, 7, 0))
-        highs = (pltpu.roll(high, 1, 0), high)
-        sums = []
-        for f in range(2):
-            before = jnp.where(even, lows[f], pltpu.roll(tiles[f][-1], 1, 0))
-            after = jnp.where(even, pltpu.roll(tiles[f][0], 7, 0), highs[f])
-            sums.append(around(tiles[f], up[f], down[f], before, after))
-        ends = [[], []]
-        for j in range(NJ):
-            at = pl.ds(j * 8, 8)
-            new_p = (
-                right[x, at, :] + coef[AP, x, at, :] * sums[0][j] + coef[BP, x, at, :] * tiles[1][j]
-            )
-            new_t = (
-                right[x, pl.ds((NJ + j) * 8, 8), :]
-                + coef[AT, x, at, :] * sums[1][j]
-                + coef[BT, x, at, :] * new_p
-            )
-            state[1 - slot, x + 1, at, :] = new_p
-            state[1 - slot, x + 1, pl.ds((NJ + j) * 8, 8), :] = new_t
-            if j in (0, NJ - 1):
-                ends[0].append(new_p)
-                ends[1].append(new_t)
-        y_message(1 - slot, x, *ends)
+    def ends_of(tiles, low, high):
+        before = jnp.where(squarter == 0, low, pltpu.roll(tiles[-1], 1, 0))
+        after = jnp.where(squarter == NQ - 1, high, pltpu.roll(tiles[0], 7, 0))
+        return before, after
+
+    def relax_rows(st, slot, n, xg):
+        low = yrecv[st, slot, 0, pl.ds(xg * 8, 8), :]
+        high = yrecv[st, slot, 1, pl.ds(xg * 8, 8), :]
+        firsts, lasts = [], []
+        for g in range(NG):
+            x = xg + g * XG
+            tiles, sums = [], []
+            for f in range(2):
+                here, up, down = (
+                    [state[st, slot, x + dx, pl.ds((f * NJ + j) * 8, 8), :] for j in range(NJ)] for dx in (1, 0, 2)
+                )
+                i = 2 * g + f
+                low_i = pltpu.roll(low, 8 - i, 0) if i else low
+                high_i = pltpu.roll(high, NQ - 1 - i, 0) if i < NQ - 1 else high
+                tiles.append(here)
+                sums.append(around(here, up, down, *ends_of(here, low_i, high_i)))
+            new = [[], []]
+            for j in range(NJ):
+                at = pl.ds(j * 8, 8)
+                at_t = pl.ds((NJ + j) * 8, 8)
+                new_p = right[st, x, at, :] + coef[n, AP, x, at, :] * sums[0][j] + coef[n, BP, x, at, :] * tiles[1][j]
+                new_t = right[st, x, at_t, :] + coef[n, AT, x, at, :] * sums[1][j] + coef[n, BT, x, at, :] * new_p
+                state[st, 1 - slot, x + 1, at, :] = new_p
+                state[st, 1 - slot, x + 1, at_t, :] = new_t
+                new[0].append(new_p)
+                new[1].append(new_t)
+            for f in range(2):
+                firsts.append(new[f][0])
+                lasts.append(new[f][-1])
+        y_message(st, 1 - slot, xg, firsts, lasts)
 
     base_cell = (lgx * NX) * (ngy * NY) + gy * NY
 
@@ -318,7 +343,7 @@
         )
 
     def repeat(ref, lead, h, value):
-        for o in range(NO):
+        for o in range(SO):
             ref[(*lead, pl.ds(o * NY + h * 8, 8), slice(None))] = value
 
     def prepare(n):
@@ -346,18 +371,14 @@
                 coupling = 0.2 * jnp.tanh(pore)
                 inv_p = 1.0 / (store_p + 6.0 * perm)
                 inv_t = 1.0 / (store_t + 12.0)
-                rows = {
-                    0: perm * inv_p,
-                    1: coupling * inv_p,
-                    2: 2.0 * inv_t,
-                    3: coupling * inv_t,
-                    4: store_p * inv_p,
-                    5: inv_p,
-                    6: store_t * inv_t,
-                    7: perm,
-                }
-                for c, value in rows.items():
-                    repeat(crep, (c, x), h, value)
+                repeat(crep, (AP, x), h, perm * inv_p)
+                repeat(crep, (BP, x), h, coupling * inv_p)
+                repeat(crep, (AT, x), h, 2.0 * inv_t)
+                repeat(crep, (BT, x), h, coupling * inv_t)
+                repeat(crep, (RPC, x), h, store_p * inv_p)
+                repeat(crep, (IP, x), h, inv_p)
+                repeat(crep, (RTC, x), h, store_t * inv_t)
+                repeat(crep, (KK, x), h, perm)
                 repeat(prep_pore, (x + 1,), h, pore)
                 ypore[n, pl.ds(x * NY + h * 8, 8), :] = pore
         for side, y in ((0, 0), (1, NY - 1)):
@@ -368,28 +389,33 @@
             def _(k=k):
                 pore_halo(n, k).start()
 
-        source = meta_in[n]
-        cell = meta_in[3] - (8 * (sub % 2) + base_cell).astype(F32)
-
         def spread(x, _):
+            for c in range(8):
+                for j in range(NJ):
+                    coef[n, c, x, pl.ds(j * 8, 8), :] = crep[c, x, pl.ds(j, 8, stride=NJ), :]
+            return 0
+
+        lax.fori_loop(0, NX, spread, 0)
+
+    def right_sides(st, n):
+        source = meta_in[st, n]
+        cell = meta_in[st, 3] - (NJ * squarter + base_cell).astype(F32)
+
+        def row(x, _):
             for j in range(NJ):
                 at = pl.ds(j * 8, 8)
-                for c in range(4):
-                    coef[c, x, at, :] = crep[c, x, pl.ds(j, 8, stride=8), :]
+                at_t = pl.ds((NJ + j) * 8, 8)
                 mine = cell == (x * (ngy * NY) + j).astype(F32)
                 term = jnp.where(mine, source, 0.0)
-                right[x, at, :] = (
-                    crep[4, x, pl.ds(j, 8, stride=8), :] * state[0, x + 1, at, :]
-                    + crep[5, x, pl.ds(j, 8, stride=8), :] * term
+                right[st, x, at, :] = (
+                    coef[n, RPC, x, at, :] * state[st, 0, x + 1, at, :] + coef[n, IP, x, at, :] * term
                 )
-                right[x, pl.ds((NJ + j) * 8, 8), :] = (
-                    crep[6, x, pl.ds(j, 8, stride=8), :] * state[0, x + 1, pl.ds((NJ + j) * 8, 8), :]
-                )
+                right[st, x, at_t, :] = coef[n, RTC, x, at, :] * state[st, 0, x + 1, at_t, :]
             return 0
 
-        lax.fori_loop(0, NX, spread, 0)
-
-    def add_gradient(n):
+        lax.fori_loop(0, NX, row, 0)
+
+    def gradient_factor(n):
         for k in range(4):
 
             @pl.when(exists[k])
@@ -400,23 +426,28 @@
         for side, row in ((0, 0), (1, NX + 1)):
             for h in range(2):
                 repeat(prep_pore, (row,), h, prow[n, side, pl.ds(h * 8, 8), :])
-        weight = meta_in[4]
 
         def row(x, _):
             tiles, up, down = (
-                [prep_pore[x + dx, pl.ds(j, 8, stride=8), :] for j in range(NJ)] for dx in (1, 0, 2)
+                [prep_pore[x + dx, pl.ds(j, 8, stride=NJ), :] for j in range(NJ)] for dx in (1, 0, 2)
             )
             low = jnp.broadcast_to(pcol[n, 0, pl.ds(x, 1), :], (8, NZ))
             high = jnp.broadcast_to(pcol[n, 1, pl.ds(x, 1), :], (8, NZ))
-            before = jnp.where(even, low, pltpu.roll(tiles[-1], 1, 0))
-            after = jnp.where(even, pltpu.roll(tiles[0], 7, 0), high)
-            sums = around(tiles, up, down, before, after)
+            sums = around(tiles, up, down, *ends_of(tiles, low, high))
             for j in range(NJ):
                 at = pl.ds(j * 8, 8)
-                laplace = sums[j] - 6.0 * tiles[j]
-                gacc[x, at, :] += (
-                    crep[7, x, pl.ds(j, 8, stride=8), :] * laplace * (weight * state[0, x + 1, at, :])
-                )
+                coef[n, KK, x, at, :] = coef[n, KK, x, at, :] * (sums[j] - 6.0 * tiles[j])
+            return 0
+
+        lax.fori_loop(0, NX, row, 0)
+
+    def add_gradient(st, n):
+        weight = meta_in[st, 4]
+
+        def row(x, _):
+            for j in range(NJ):
+                at = pl.ds(j * 8, 8)
+                gacc[x, at, :] += coef[n, KK, x, at, :] * (weight * state[st, 0, x + 1, at, :])
             return 0
 
         lax.fori_loop(0, NX, row, 0)
@@ -436,65 +467,76 @@
             outst.at[:, pl.ds(k * NY, NY), :], out_ref.at[k // NO, k % NO], orecv.at[k]
         )
 
-    def finish():
+    def finish(st):
         def row(x, _):
             for f in range(2):
-                for o in range(NO):
-                    for h in range(2):
-                        outst[x, pl.ds((f * NO + o) * NY + h * 8, 8), :] = state[
-                            0, x + 1, pl.ds(f * 64 + 2 * o + h, 8, stride=8), :
-                        ]
+                for j in range(NJ):
+                    outst[x, pl.ds((f * NO + st * SO) * NY + j, 8, stride=NJ), :] = state[
+                        st, 0, x + 1, pl.ds((f * NJ + j) * 8, 8), :
+                    ]
             return 0
 
         lax.fori_loop(0, NX, row, 0)
 
         @pl.when(moves)
         def _():
-            for k in range(2 * NO):
+            for k in streams_obs(st):
                 swap_out(k).start()
 
         @pl.when(stays)
         def _():
-            for k in range(2 * NO):
+            for k in streams_obs(st):
                 keep_out(k).start()
 
+    def iterate(st, k):
+        n, slot = NS - 1 - k // ITERS, k % 2
+        if k % ITERS == 0:
+            right_sides(st, n)
+        wait_halos(st, slot)
+
+        def rows(xg, _):
+            relax_rows(st, slot, n, xg)
+            return 0
+
+        lax.fori_loop(0, XG, rows, 0, unroll=UNROLL)
+        if k < NS * ITERS - 1:
+            start_halos(st, 1 - slot)
+        else:
+            finish(st)
+        if k % ITERS == ITERS - 1:
+            add_gradient(st, n)
+
     gacc[...] = jnp.zeros(gacc.shape, F32)
-
-    def step(i, _):
-        n = NS - 1 - i
-        prepare(n)
-        for sweep in range(ITERS):
-            slot = sweep % 2
-            wait_halos(slot)
-
-            def row(x, _, slot=slot):
-                relax_row(slot, x, False)
-                return 0
-
-            lax.fori_loop(0, NX, row, 0, unroll=2)
-            if sweep < ITERS - 1:
-                start_halos(1 - slot)
-
-        @pl.when(n > 0)
-        def _():
-            start_halos(0)
-
-        @pl.when(n == 0)
-        def _():
-            finish()
-
-        add_gradient(n)
-        return 0
-
-    lax.fori_loop(0, NS, step, 0)
-
+    set_up(0)
+
+    @pl.when(moves)
+    def _():
+        send_meta().wait()
+
+    prepare(NS - 1)
+    for k in range(NS * ITERS + ST - 1):
+        n = NS - 1 - k // ITERS
+        if k % ITERS == 0 and 0 < k < NS * ITERS:
+            prepare(n)
+        if k % ITERS == ITERS - 1:
+            gradient_factor(n)
+        if k < ST:
+            if k > 0:
+                set_up(k)
+        for st in range(ST):
+            if 0 <= k - st < NS * ITERS:
+                iterate(st, k - st)
+        if k < NS - 1:
+            send_saved(NS - 2 - k)
+
+    for x in range(NX):
+        for j in range(NJ):
+            total = gacc[x, pl.ds(j * 8, 8), :]
+            for o in range(1, SO):
+                total = total + pltpu.roll(gacc[x, pl.ds(j * 8, 8), :], NQ * o, 0)
+            gsum[x, pl.ds(j, 8, stride=NJ), :] = total
     for h in range(2):
-        whole = []
-        for x in range(NX):
-            total = gacc[x, pl.ds(h, 8, stride=8), :]
-            for o in range(1, NO):
-                total = total + gacc[x, pl.ds(2 * o + h, 8, stride=8), :]
-            whole.append(total)
+        whole = [gsum[x, pl.ds(h * 8, 8), :] for x in range(NX)]
         for d, tile in enumerate(regroup(whole, lane_group)):
             gpack[d, pl.ds(h * 8, 8), :] = tile
 
@@ -568,7 +610,6 @@
     vmem = pl.BlockSpec(memory_space=pltpu.VMEM)
     smem = pl.BlockSpec(memory_space=pltpu.SMEM)
     dma = pltpu.SemaphoreType.DMA
-    rows = 2 * NJ * 8
     return pl.pallas_call(
         kernel,
         out_shape=(
@@ -581,32 +622,33 @@
             pltpu.VMEM((NS, 4, NX, NY, LP), F32),
             pltpu.VMEM((NS, 64, NZ), F32),
             pltpu.VMEM((NS, NP, 64, NZ), F32),
-            pltpu.VMEM((NX, rows, NZ), F32),
-            pltpu.VMEM((5, 8, NZ), F32),
-            pltpu.VMEM((5, 8, NZ), F32),
-            pltpu.VMEM((2, NX + 2, rows, NZ), F32),
-            pltpu.VMEM((2, 2, NX * 8, NZ), F32),
-            pltpu.VMEM((2, 2, NX * 8, NZ), F32),
-            pltpu.VMEM((4, NX, 64, NZ), F32),
-            pltpu.VMEM((8, NX, 64, NZ), F32),
-            pltpu.VMEM((NX + 2, 64, NZ), F32),
+            pltpu.VMEM((NX, 2 * NO * NY, NZ), F32),
+            pltpu.VMEM((ST, 5, 8, NZ), F32),
+            pltpu.VMEM((ST, 5, 8, NZ), F32),
+            pltpu.VMEM((ST, 2, NX + 2, ROWS, NZ), F32),
+            pltpu.VMEM((ST, 2, 2, XG * 8, NZ), F32),
+            pltpu.VMEM((ST, 2, 2, XG * 8, NZ), F32),
+            pltpu.VMEM((NS, 8, NX, NJ * 8, NZ), F32),
+            pltpu.VMEM((8, NX, SO * NY, NZ), F32),
+            pltpu.VMEM((NX + 2, SO * NY, NZ), F32),
             pltpu.VMEM((NS, NX * NY, NZ), F32),
             pltpu.VMEM((NS, 2, 8, NZ), F32),
             pltpu.VMEM((NS, 2, NY, NZ), F32),
             pltpu.VMEM((NS, 2, 8, NZ), F32),
-            pltpu.VMEM((NX, rows, NZ), F32),
-            pltpu.VMEM((NX, 64, NZ), F32),
+            pltpu.VMEM((ST, NX, ROWS, NZ), F32),
+            pltpu.VMEM((NX, NJ * 8, NZ), F32),
+            pltpu.VMEM((NX, 8 * NJ, NZ), F32),
             pltpu.VMEM((NP, NY, NZ), F32),
             pltpu.VMEM((NP, NY, NZ), F32),
-            pltpu.VMEM((NX, rows, NZ), F32),
+            pltpu.VMEM((NX, 2 * NO * NY, NZ), F32),
             dma((NS, 4)),
             dma((NS, NP)),
             dma((NS, NP)),
             dma((2 * NO,)),
             dma((2 * NO,)),
             dma((2,)),
-            dma((2, 4)),
-            dma((2, 4)),
+            dma((ST, 2, 4)),
+            dma((ST, 2, 4)),
             dma((NS, 4)),
             dma((NS, 4)),
             dma((2 * NO,)),

time: 95.8 us -> 80.8 us (0.84)
  Pallas kernels: 86.7 us -> 71.7 us
    pallas_call x1, Pallas kernels: 86.7 us -> 71.7 us  [local(): pl.pallas_call(kernel, out_shape=(jax.ShapeDtypeStruct((2, NO, NX, NY, NZ...]
where the time goes in v2:
time: 80.8 us; the launch traced here: 80.5 us
  Pallas kernels  71.7 us (89%)
  local copies, waits for them, and re-layouts  8.17 us (10%)
    pallas_call x1, Pallas kernels, local(): pl.pallas_call(kernel, out_shape=(jax.ShapeDtypeStruct((2, NO, NX, NY, NZ...  71.7 us
    unnamed x18, local copies, waits for them, and re-layouts  8.17 us

profile of v2, /device:TPU:1, one launch (start us, length us, event | category | flops | bytes accessed | tf_op | source)
XLA Modules:
  0.0 80.5 jit_solution(12744992543345189237)
XLA Ops:
  0.6 0.0 copy-start
  0.6 1.0 %copy-done = f32[2,4,8,16,128]{4,3,2,1,0:T(8,128)S(1)} copy-done((f32[2,4,8,16,128]{4,3,2,1,0:T(8,128)S(1)}, f32[2,4,8,16,128]{4,3,2,1,0:T(8,128)}, u32[]{:S(2)}) %copy-start) | copy-done | bytes 524312
  1.7 0.0 copy-start.1
  1.7 0.9 %copy-done.1 = f32[3,8,16,16]{3,2,1,0:T(8,128)S(1)} copy-done((f32[3,8,16,16]{3,2,1,0:T(8,128)S(1)}, f32[3,8,16,16]{3,2,1,0:T(8,128)}, u32[]{:S(2)}) %copy-start.1) | copy-done | bytes 24600
  2.6 0.0 copy-start.2
  2.6 0.9 %copy-done.2 = f32[3,8,16,16]{3,2,1,0:T(8,128)S(1)} copy-done((f32[3,8,16,16]{3,2,1,0:T(8,128)S(1)}, f32[3,8,16,16]{3,2,1,0:T(8,128)}, u32[]{:S(2)}) %copy-start.2) | copy-done | bytes 24600
  3.5 0.0 copy-start.3
  3.5 0.9 %copy-done.3 = f32[3,8,16,16]{3,2,1,0:T(8,128)S(1)} copy-done((f32[3,8,16,16]{3,2,1,0:T(8,128)S(1)}, f32[3,8,16,16]{3,2,1,0:T(8,128)}, u32[]{:S(2)}) %copy-start.3) | copy-done | bytes 24600
  4.5 0.0 copy-start.4
  4.5 0.9 %copy-done.4 = f32[3,8,16,16]{3,2,1,0:T(8,128)S(1)} copy-done((f32[3,8,16,16]{3,2,1,0:T(8,128)S(1)}, f32[3,8,16,16]{3,2,1,0:T(8,128)}, u32[]{:S(2)}) %copy-start.4) | copy-done | bytes 24600
  5.4 0.0 copy-start.5
  5.4 0.7 copy-done.5
  6.1 0.0 copy-start.6
  6.1 0.7 copy-done.6
  6.7 0.0 copy-start.7
  6.7 0.7 copy-done.7
  7.4 71.7 %shard_map.95 = (f32[2,4,8,16,128]{4,3,2,1,0:T(8,128)S(1)}, f32[8,16,16]{2,1,0:T(8,128)S(1)}) custom-call(f32[2,4,8,16,128]{4,3,2,1,0:T(8,128)S(1)} %copy-done, f32[3,8,16,16]{3,2,1,0:T(8,128)S(1)} %copy-done.1, f32[3,8,16,16]{3,2,1,0:T(8,128)S(1)} %copy-done.2, f32[3,8,16,16]{3,2,1,0:T(8,128)S(1)} %copy-done.3, f32[3,8,16,16]{3,2,1,0:T(8,128)S(1)} %copy-done.4, ...), custom_call_target="tpu_custom_call" | custom-call | tf_op jit(solution)/shard_map/pallas_call | solution.py:613
  79.1 0.8 copy.12
  79.9 0.6 copy.13
Async XLA Ops:
  0.6 1.0 %copy-start = (f32[2,4,8,16,128]{4,3,2,1,0:T(8,128)S(1)}, f32[2,4,8,16,128]{4,3,2,1,0:T(8,128)}, u32[]{:S(2)}) copy-start(f32[2,4,8,16,128]{4,3,2,1,0:T(8,128)} %cost_ref.1) | copy-start | bytes 1572868
  1.7 0.9 %copy-start.1 = (f32[3,8,16,16]{3,2,1,0:T(8,128)S(1)}, f32[3,8,16,16]{3,2,1,0:T(8,128)}, u32[]{:S(2)}) copy-start(f32[3,8,16,16]{3,2,1,0:T(8,128)} %pore_ref.1) | copy-start | bytes 73732
  2.6 0.9 %copy-start.2 = (f32[3,8,16,16]{3,2,1,0:T(8,128)S(1)}, f32[3,8,16,16]{3,2,1,0:T(8,128)}, u32[]{:S(2)}) copy-start(f32[3,8,16,16]{3,2,1,0:T(8,128)} %heat_ref.1) | copy-start | bytes 73732
  3.5 0.9 %copy-start.3 = (f32[3,8,16,16]{3,2,1,0:T(8,128)S(1)}, f32[3,8,16,16]{3,2,1,0:T(8,128)}, u32[]{:S(2)}) copy-start(f32[3,8,16,16]{3,2,1,0:T(8,128)} %dil_ref.1) | copy-start | bytes 73732
  4.5 0.9 %copy-start.4 = (f32[3,8,16,16]{3,2,1,0:T(8,128)S(1)}, f32[3,8,16,16]{3,2,1,0:T(8,128)}, u32[]{:S(2)}) copy-start(f32[3,8,16,16]{3,2,1,0:T(8,128)} %cond_ref.1) | copy-start | bytes 73732
  5.4 0.7 copy-start.5
  6.1 0.7 copy-start.6
  6.7 0.7 copy-start.7

commit v3 on v2

--- a/solution.py
+++ b/solution.py
@@ -10,7 +10,7 @@
 MESH = pl.DeviceIdType.MESH
 F32 = jnp.float32
 ITERS = 4
-UNROLL = 2
+UNROLL = 4
 NX, NY, NZ = 8, 16, 128
 NS = 3
 NO = 4
@@ -657,7 +657,7 @@
             dma((NP,)),
         ],
         compiler_params=pltpu.CompilerParams(
-            collective_id=0, has_side_effects=True, vmem_limit_bytes=48 * 1024 * 1024
+            collective_id=0, has_side_effects=True, vmem_limit_bytes=67043328
         ),
     )(*args)
 

time: 80.8 us -> 74 us (0.916)
  local copies, waits for them, and re-layouts: 8.17 us -> 2.53 us
  Pallas kernels: 71.7 us -> 70.6 us
    unnamed x18 -> x4, local copies, waits for them, and re-layouts: 8.17 us -> 2.53 us
    pallas_call x1, Pallas kernels: 71.7 us -> 70.6 us  [local(): pl.pallas_call(kernel, out_shape=(jax.ShapeDtypeStruct((2, NO, NX, NY, NZ...]
where the time goes in v3:
time: 74 us; the launch traced here: 73.8 us
  Pallas kernels  70.6 us (95%)
  local copies, waits for them, and re-layouts  2.53 us (3%)
    pallas_call x1, Pallas kernels, local(): pl.pallas_call(kernel, out_shape=(jax.ShapeDtypeStruct((2, NO, NX, NY, NZ...  70.6 us
    unnamed x4, local copies, waits for them, and re-layouts  2.53 us

profile of v3, /device:TPU:1, one launch (start us, length us, event | category | flops | bytes accessed | tf_op | source)
XLA Modules:
  0.0 73.8 jit_solution(71186604751894068)
XLA Ops:
  0.6 70.6 %shard_map.95 = (f32[2,4,8,16,128]{4,3,2,1,0:T(8,128)}, f32[8,16,16]{2,1,0:T(8,128)}) custom-call(f32[2,4,8,16,128]{4,3,2,1,0:T(8,128)} %cost_ref.1, f32[3,8,16,16]{3,2,1,0:T(8,128)} %pore_ref.1, f32[3,8,16,16]{3,2,1,0:T(8,128)} %heat_ref.1, f32[3,8,16,16]{3,2,1,0:T(8,128)} %dil_ref.1, f32[3,8,16,16]{3,2,1,0:T(8,128)} %cond_ref.1, f32[3,4,128]{2,1,0:T(4,128)} %resid_ref.1, ...), custom_call_target="tpu_custom_call" | custom-call | tf_op jit(solution)/shard_map/pallas_call | solution.py:613
  71.2 0.0 copy-start
  71.2 1.9 %copy.12 = f32[2,4,8,16,128]{4,3,2,1,0:T(8,128)} copy(f32[2,4,8,16,128]{4,3,2,1,0:T(8,128)} %get-tuple-element.4) | data formatting | bytes 1048576
  73.2 0.0 copy-done
  73.2 0.6 copy.13
Async XLA Ops:
  71.2 1.9 %copy-start = (f32[8,16,16]{2,1,0:T(8,128)S(1)}, f32[8,16,16]{2,1,0:T(8,128)}, u32[]{:S(2)}) copy-start(f32[8,16,16]{2,1,0:T(8,128)} %get-tuple-element.5) | copy-start | bytes 24580

commit v4 on v3

v4 whole, which is shorter than its diff:
```python
import functools

import jax
import jax.numpy as jnp
from jax import lax
from jax.experimental import pallas as pl
from jax.experimental.pallas import tpu as pltpu
from jax.sharding import PartitionSpec as P

MESH = pl.DeviceIdType.MESH
F32 = jnp.float32
ITERS = 4
LAG = 0
UNROLL = 4
NX, NY, NZ = 8, 16, 128
NS = 3
NO = 4
NP = 8
LP = NZ // NP
SO = 2
ST = NO // SO
NQ = 8 // SO
NJ = NY // NQ
NG = NQ // 2
XG = NX // NG
ROWS = 2 * NJ * 8
NE = NJ + 2
ROUNDS = NS * ITERS // 2
AP, BP, AT, BT, RPC, IP, RTC, KK = range(8)


PLAN = {
    "start": (("forward", 2), ("send", 1), ("prepare", 2), ("set_up", 0), ("set_up", 1), ("complete", 2)),
    (0, 0): (("forward", 1),),
    (1, 0): (("prepare", 1),),
    (1, 1): (("complete", 1), ("send", 0)),
    (2, 1): (("forward", 0),),
    (3, 0): (("prepare", 0),),
    (3, 1): (("complete", 0),),
}


def role(obs, gx):
    return 2 * (obs // 2) + gx % 2, 2 * (gx // 2) + obs % 2


def regroup(tiles, lane_group):
    turned = [pltpu.roll(t, LP * d, 1) if d else t for d, t in enumerate(tiles)]
    outs = []
    for x in range(NP):
        mixed = turned[(NP - 1 - x) % NP]
        for g in range(NP - 1):
            mixed = jnp.where(lane_group == g, turned[(g - x) % NP], mixed)
        outs.append(pltpu.roll(mixed, NZ - LP * x, 1) if x else mixed)
    return outs


def kernel(
    cost_ref, pore_ref, heat_ref, dil_ref, cond_ref, resid_ref, pos_ref, wgt_ref,
    out_ref, grad_ref,
    saved, pack, gath, raw, meta, meta_in, state, mid, edge, ysend, yrecv, corner,
    coef, crep, ccol, prep_pore, yfield, ycol, prow, pcol, right, gacc, gsum, gpack, gred, outst,
    load_sem, gsend, grecv, gfwd, ssend, srecv, msem, hsend, hrecv, csend, crecv, psend, precv, osend, orecv, rsend, rrecv,
):
    obs, gx, gy = lax.axis_index("obs"), lax.axis_index("gx"), lax.axis_index("gy")
    lobs, lgx = role(obs, gx)
    stays = jnp.logical_and(lobs == obs, lgx == gx)
    moves = jnp.logical_not(stays)
    zh, yy = obs // 2, gx // 2
    ngx, ngy = lax.axis_size("gx"), lax.axis_size("gy")

    lane = lax.broadcasted_iota(jnp.int32, (8, NZ), 1)
    sub = lax.broadcasted_iota(jnp.int32, (8, NZ), 0)
    lane_group = lane // LP
    first_lane, last_lane = lane == 0, lane == NZ - 1

    exists = (lgx > 0, lgx < ngx - 1, gy > 0, gy < ngy - 1)
    xm = role(lobs, jnp.maximum(lgx - 1, 0))
    xp = role(lobs, jnp.minimum(lgx + 1, ngx - 1))
    near = (
        (xm[0], xm[1], gy),
        (xp[0], xp[1], gy),
        (obs, gx, jnp.maximum(gy - 1, 0)),
        (obs, gx, jnp.minimum(gy + 1, ngy - 1)),
    )
    slant_exists = [jnp.logical_and(exists[cx], exists[2 + cy]) for cx in range(2) for cy in range(2)]
    slant = [(near[cx][0], near[cx][1], near[2 + cy][2]) for cx in range(2) for cy in range(2)]
    partner = (lobs, lgx, gy)

    fields = (pore_ref, heat_ref, dil_ref, cond_ref)

    def load(n, f):
        return pltpu.make_async_copy(fields[f].at[n], saved.at[n, f], load_sem.at[n, f])

    for n in range(NS - 1, -1, -1):
        for f in range(4):
            load(n, f).start()

    zero = jnp.zeros((8, NZ), F32)
    for st in range(ST):
        for par in range(2):
            for row in (0, 1, NX + 2, NX + 3):
                state[st, par, row] = jnp.zeros((ROWS, NZ), F32)
    yrecv[...] = jnp.zeros(yrecv.shape, F32)
    corner[...] = jnp.zeros(corner.shape, F32)
    prow[...] = jnp.zeros(prow.shape, F32)
    pcol[...] = jnp.zeros(pcol.shape, F32)

    barrier = pltpu.get_barrier_semaphore()
    for zz in range(4):
        for core in range(2):
            for low in range(2):
                there = (2 * zz + core, 2 * yy + low, gy)

                @pl.when(jnp.logical_or(there[0] != obs, there[1] != gx))
                def _(there=there):
                    pl.semaphore_signal(barrier, inc=1, device_id=there, device_id_type=MESH)

    for k in range(4):

        @pl.when(exists[k])
        def _(k=k):
            pl.semaphore_signal(barrier, inc=1, device_id=near[k], device_id_type=MESH)

        @pl.when(slant_exists[k])
        def _(k=k):
            pl.semaphore_signal(barrier, inc=1, device_id=slant[k], device_id_type=MESH)

    count = 15
    for k in range(4):
        count = count + exists[k].astype(jnp.int32) + slant_exists[k].astype(jnp.int32)
    pl.semaphore_wait(barrier, count)

    srow = sub // NQ
    squarter = sub % NQ
    for st in range(ST):
        for n in range(NS):
            tile = zero
            for o in range(SO):
                k = st * SO + o
                tile = jnp.where(srow == o, jnp.broadcast_to(resid_ref[n, k : k + 1, :], (8, NZ)), tile)
            meta[st, n] = tile
        pos = jnp.zeros((8, NZ), jnp.int32)
        wgt = jnp.zeros((8, NZ), jnp.int32)
        for o in range(SO):
            pos = jnp.where(srow == o, pos_ref[st * SO + o], pos)
            wgt = jnp.where(srow == o, wgt_ref[st * SO + o], wgt)
        meta[st, 3] = pos.astype(F32)
        meta[st, 4] = wgt.astype(F32)

    def gather_copy(n, zt):
        return pltpu.make_async_remote_copy(
            src_ref=pack.at[n],
            dst_ref=gath.at[n, obs],
            send_sem=gsend.at[n, zt],
            recv_sem=grecv.at[n, obs],
            device_id=(2 * zt + gx % 2, gx, gy),
            device_id_type=MESH,
        )

    zl = gx % 2
    onward = (2 * lax.rem(zh + 3 + 2 * zl, 4) + zl, 2 * yy + 1 - zl, gy)

    def forward_copy(n, d):
        return pltpu.make_async_remote_copy(
            src_ref=gath.at[n, d],
            dst_ref=gath.at[n, d],
            send_sem=gfwd.at[n, d],
            recv_sem=grecv.at[n, d],
            device_id=onward,
            device_id_type=MESH,
        )

    def forward(n):
        @pl.when(stays)
        def _():
            for off in (0, 1, 3, 2):
                for core in range(2):
                    d = 2 * lax.rem(zh + off, 4) + core
                    if off == 0:

                        @pl.when(obs != d)
                        def _(d=d):
                            forward_copy(n, d).wait_recv()

                    else:
                        forward_copy(n, d).wait_recv()
                    forward_copy(n, d).start()

    def is_me(target):
        return jnp.logical_and(stays, lobs == target)

    def send_saved(n):
        for f in range(4):
            load(n, f).wait()
        for f in range(4):
            for h in range(2):
                packed = saved_tile(n, f, 0, h)
                for x in range(1, NX):
                    packed = jnp.where(
                        lane_group == x, pltpu.roll(saved_tile(n, f, x, h), LP * x, 1), packed
                    )
                pack[n, pl.ds((f * 2 + h) * 8, 8), :] = packed

                @pl.when(stays)
                def _(packed=packed, f=f, h=h):
                    gath[n, obs, pl.ds((f * 2 + h) * 8, 8), :] = packed

        for zt in range(4):

            @pl.when(jnp.logical_not(jnp.logical_and(stays, zh == zt)))
            def _(zt=zt):
                gather_copy(n, zt).start()

    def saved_tile(n, f, x, h):
        piece = saved[n, f, x, pl.ds(h * 8, 8), :]
        return jnp.concatenate([piece, jnp.zeros((8, NZ - LP), F32)], axis=1)

    def swap_in(k):
        return pltpu.make_async_remote_copy(
            src_ref=cost_ref.at[k // NO, k % NO],
            dst_ref=raw.at[:, pl.ds(k * NY, NY), :],
            send_sem=ssend.at[k],
            recv_sem=srecv.at[k],
            device_id=partner,
            device_id_type=MESH,
        )

    def keep_in(k):
        return pltpu.make_async_copy(
            cost_ref.at[k // NO, k % NO], raw.at[:, pl.ds(k * NY, NY), :], srecv.at[k]
        )

    def send_meta():
        return pltpu.make_async_remote_copy(
            src_ref=meta, dst_ref=meta_in, send_sem=msem.at[0], recv_sem=msem.at[1], device_id=partner, device_id_type=MESH
        )

    def streams_obs(st):
        return [f * NO + st * SO + o for f in range(2) for o in range(SO)]

    send_saved(NS - 1)

    @pl.when(moves)
    def _():
        send_meta().start()
        for st in range(ST):
            for k in streams_obs(st):
                swap_in(k).start()

    @pl.when(stays)
    def _():
        for st in range(ST):
            for k in streams_obs(st):
                keep_in(k).start()
        meta_in[...] = meta[...]

    def halo(st, par, k):
        if k == 0:
            src, dst = state.at[st, par, pl.ds(2, 2)], state.at[st, par, pl.ds(NX + 2, 2)]
        elif k == 1:
            src, dst = state.at[st, par, pl.ds(NX, 2)], state.at[st, par, pl.ds(0, 2)]
        elif k == 2:
            src, dst = ysend.at[st, par, 0], yrecv.at[st, par, 1]
        else:
            src, dst = ysend.at[st, par, 1], yrecv.at[st, par, 0]
        return pltpu.make_async_remote_copy(
            src_ref=src,
            dst_ref=dst,
            send_sem=hsend.at[st, par, k],
            recv_sem=hrecv.at[st, par, k ^ 1],
            device_id=near[k],
            device_id_type=MESH,
        )

    def corner_copy(st, par, k):
        cx, cy = k // 2, k % 2
        return pltpu.make_async_remote_copy(
            src_ref=ysend.at[st, par, cy, 0, pl.ds((XG - 1) * 8 if cx else 0, 8)],
            dst_ref=corner.at[st, par, 3 - k],
            send_sem=csend.at[st, par, k],
            recv_sem=crecv.at[st, par, 3 - k],
            device_id=slant[k],
            device_id_type=MESH,
        )

    def start_halos(st, par):
        for k in range(4):

            @pl.when(slant_exists[k])
            def _(k=k):
                corner_copy(st, par, k).start()

        for k in range(4):

            @pl.when(exists[k])
            def _(k=k):
                halo(st, par, k).start()

    def wait_sent(st, par):
        for k in range(4):

            @pl.when(exists[k])
            def _(k=k):
                halo(st, par, k).wait_send()

            @pl.when(slant_exists[k])
            def _(k=k):
                corner_copy(st, par, k).wait_send()

    def wait_halos(st, par):
        for k in range(4):

            @pl.when(exists[k])
            def _(k=k):
                halo(st, par, k ^ 1).wait_recv()

            @pl.when(slant_exists[k])
            def _(k=k):
                corner_copy(st, par, 3 - k).wait_recv()

    def y_message(st, par, xg, firsts, lasts):
        for col in range(2):
            low, high = firsts[0][col], pltpu.roll(lasts[0][col], (9 - NQ) % 8, 0)
            for i in range(1, NQ):
                low = jnp.where(squarter == i, pltpu.roll(firsts[i][col], i, 0), low)
                turned = lasts[i][col] if i == NQ - 1 else pltpu.roll(lasts[i][col], (9 + i - NQ) % 8, 0)
                high = jnp.where(squarter == i, turned, high)
            ysend[st, par, 0, col, pl.ds(xg * 8, 8), :] = low
            ysend[st, par, 1, col, pl.ds(xg * 8, 8), :] = high

    def core(f, j):
        return pl.ds((f * NJ + j) * 8, 8)

    def ext(f, j):
        return pl.ds((f * NE + j + 1) * 8, 8)

    def set_up(st):
        @pl.when(moves)
        def _():
            for k in streams_obs(st):
                swap_in(k).wait()

        @pl.when(stays)
        def _():
            for k in streams_obs(st):
                keep_in(k).wait()

        def first_rows(xg, _):
            firsts, lasts = [], []
            for g in range(NG):
                x = xg + g * XG
                for f in range(2):
                    start = (f * NO + st * SO) * NY
                    tiles = [raw[x, pl.ds(start + j, 8, stride=NJ), :] for j in range(NJ)]
                    for j in range(NJ):
                        state[st, 0, x + 2, core(f, j), :] = tiles[j]
                    firsts.append(tiles[:2])
                    lasts.append((tiles[-1], tiles[-2]))
            y_message(st, 0, xg, firsts, lasts)
            return 0

        lax.fori_loop(0, XG, first_rows, 0)
        start_halos(st, 0)

    def around(tiles, up, down):
        sums = []
        for j, (above, below) in enumerate(zip(up, down)):
            here = tiles[j + 1]
            total = above + below + tiles[j] + tiles[j + 2]
            deep = jnp.where(first_lane, 0.0, pltpu.roll(here, 1, 1))
            shallow = jnp.where(last_lane, 0.0, pltpu.roll(here, NZ - 1, 1))
            sums.append(total + deep + shallow)
        return sums

    def before_of(inner, outside):
        return jnp.where(squarter == 0, outside, pltpu.roll(inner, 1, 0))

    def after_of(inner, outside):
        return jnp.where(squarter == NQ - 1, outside, pltpu.roll(inner, 7, 0))

    def slot_low(tile, i):
        return pltpu.roll(tile, 8 - i, 0) if i else tile

    def slot_high(tile, i):
        return pltpu.roll(tile, NQ - 1 - i, 0) if i < NQ - 1 else tile

    def fill_edges(st, par):
        def rows(xg, _):
            lows = [yrecv[st, par, 0, col, pl.ds(xg * 8, 8), :] for col in range(2)]
            highs = [yrecv[st, par, 1, col, pl.ds(xg * 8, 8), :] for col in range(2)]
            for g in range(NG):
                x = xg + g * XG
                for f in range(2):
                    i = 2 * g + f
                    for col in range(2):
                        inner = state[st, par, x + 2, core(f, NJ - 1 - col), :]
                        edge[st, x + 1, f, 1 - col] = before_of(inner, slot_low(lows[col], i))
                        inner = state[st, par, x + 2, core(f, col), :]
                        edge[st, x + 1, f, 2 + col] = after_of(inner, slot_high(highs[col], i))
            return 0

        lax.fori_loop(0, XG, rows, 0, unroll=2)
        for cx, x, g in ((0, -1, NG - 1), (1, NX, 0)):
            for f in range(2):
                i = 2 * g + f
                inner = state[st, par, x + 2, core(f, NJ - 1), :]
                edge[st, x + 1, f, 1] = before_of(inner, slot_low(corner[st, par, 2 * cx], i))
                inner = state[st, par, x + 2, core(f, 0), :]
                edge[st, x + 1, f, 2] = after_of(inner, slot_high(corner[st, par, 2 * cx + 1], i))

    def wide(st, par, x, f, reach):
        tiles = [state[st, par, x + 2, core(f, j), :] for j in range(NJ)]
        low = [edge[st, x + 1, f, e] for e in range(2 - reach, 2)]
        high = [edge[st, x + 1, f, e] for e in range(2, 2 + reach)]
        return low + tiles + high

    def relaxed(st, n, x, j, near_p, near_t, old_t):
        at, at_t = ext(0, j), ext(1, j)
        new_p = right[st, x + 1, at, :] + coef[n, AP, x + 1, at, :] * near_p + coef[n, BP, x + 1, at, :] * old_t
        new_t = right[st, x + 1, at_t, :] + coef[n, AT, x + 1, at, :] * near_t + coef[n, BT, x + 1, at, :] * new_p
        return new_p, new_t

    def first_sweep(st, par, n):
        def row(x, reach):
            here, sums = [], []
            for f in range(2):
                tiles = wide(st, par, x, f, reach + 1)
                up, down = wide(st, par, x - 1, f, reach), wide(st, par, x + 1, f, reach)
                here.append(tiles)
                sums.append(around(tiles, up, down))
            for p in range(NJ + 2 * reach):
                j = p - reach
                new_p, new_t = relaxed(st, n, x, j, sums[0][p], sums[1][p], here[1][p + 1])
                mid[st, x + 1, ext(0, j), :] = new_p
                mid[st, x + 1, ext(1, j), :] = new_t

        def inner(x, _):
            row(x, 1)
            return 0

        lax.fori_loop(0, NX, inner, 0, unroll=UNROLL)
        row(-1, 0)
        row(NX, 0)

    def second_sweep(st, par, n, last):
        def rows(xg, _):
            firsts, lasts = [], []
            for g in range(NG):
                x = xg + g * XG
                here, sums = [], []
                for f in range(2):
                    tiles = [mid[st, x + 1, ext(f, j), :] for j in range(-1, NJ + 1)]
                    up = [mid[st, x, ext(f, j), :] for j in range(NJ)]
                    down = [mid[st, x + 2, ext(f, j), :] for j in range(NJ)]
                    here.append(tiles)
                    sums.append(around(tiles, up, down))
                new = [[], []]
                for j in range(NJ):
                    new_p, new_t = relaxed(st, n, x, j, sums[0][j], sums[1][j], here[1][j + 1])
                    state[st, 1 - par, x + 2, core(0, j), :] = new_p
                    state[st, 1 - par, x + 2, core(1, j), :] = new_t
                    new[0].append(new_p)
                    new[1].append(new_t)
                for f in range(2):
                    firsts.append(new[f][:2])
                    lasts.append((new[f][-1], new[f][-2]))
            if not last:
                y_message(st, 1 - par, xg, firsts, lasts)
            return 0

        lax.fori_loop(0, XG, rows, 0, unroll=UNROLL // 2)

    base_cell = (lgx * NX) * (ngy * NY) + gy * NY

    def field_halo(n, k):
        if k == 0:
            src, dst = yfield.at[n, :, pl.ds(0, NY)], prow.at[n, 1]
        elif k == 1:
            src, dst = yfield.at[n, :, pl.ds((NX - 1) * NY, NY)], prow.at[n, 0]
        elif k == 2:
            src, dst = ycol.at[n, 0], pcol.at[n, 1]
        else:
            src, dst = ycol.at[n, 1], pcol.at[n, 0]
        return pltpu.make_async_remote_copy(
            src_ref=src,
            dst_ref=dst,
            send_sem=psend.at[n, k],
            recv_sem=precv.at[n, k ^ 1],
            device_id=near[k],
            device_id_type=MESH,
        )

    def repeat(ref, lead, h, value):
        for o in range(SO):
            ref[(*lead, pl.ds(o * NY + h * 8, 8), slice(None))] = value

    def factors(pore, heat, dil, perm):
        store_p = jnp.exp(dil)
        store_t = jnp.exp(0.5 * heat)
        coupling = 0.2 * jnp.tanh(pore)
        inv_p = 1.0 / (store_p + 6.0 * perm)
        inv_t = 1.0 / (store_t + 12.0)
        return (
            perm * inv_p, coupling * inv_p, 2.0 * inv_t, coupling * inv_t,
            store_p * inv_p, inv_p, store_t * inv_t,
        )

    def prepare(n):
        @pl.when(moves)
        def _():
            for d in range(NP):
                forward_copy(n, d).wait_recv()

        for h in range(2):
            whole = [
                regroup([gath[n, d, pl.ds((f * 2 + h) * 8, 8), :] for d in range(NP)], lane_group) for f in range(4)
            ]
            for f in range(4):
                for x in range(NX):
                    yfield[n, f, pl.ds(x * NY + h * 8, 8), :] = whole[f][x]
        for f in range(4):
            for side, y in ((0, 0), (1, NY - 1)):
                ycol[n, side, f] = yfield[n, f, pl.ds(y, NX, stride=NY), :]
        for k in range(4):

            @pl.when(exists[k])
            def _(k=k):
                field_halo(n, k).start()

        def row(x, _):
            for h in range(2):
                values = [yfield[n, f, pl.ds(pl.multiple_of(x * NY + h * 8, 8), 8), :] for f in range(4)]
                for c, value in enumerate(factors(*values)):
                    repeat(crep, (c, x + 1), h, value)
                repeat(crep, (KK, x + 1), h, values[3])
                repeat(prep_pore, (x + 1,), h, values[0])
            return 0

        lax.fori_loop(0, NX, row, 0, unroll=2)

    def complete(n):
        for k in range(4):

            @pl.when(exists[k])
            def _(k=k):
                field_halo(n, k ^ 1).wait_recv()
                field_halo(n, k).wait_send()

        for side, x in ((0, -1), (1, NX)):
            for h in range(2):
                values = [prow[n, side, f, pl.ds(h * 8, 8), :] for f in range(4)]
                for c, value in enumerate(factors(*values)):
                    repeat(crep, (c, x + 1), h, jnp.where(exists[side], value, 0.0))
                repeat(prep_pore, (x + 1,), h, values[0])
            values = [pcol[n, side, f] for f in range(4)]
            for c, value in enumerate(factors(*values)):
                ccol[c, side] = jnp.where(exists[2 + side], value, 0.0)

        def tiles_of(c, x):
            tiles = [crep[c, x + 1, pl.ds(j, 8, stride=NJ), :] for j in range(NJ)]
            for j in range(NJ):
                coef[n, c, x + 1, ext(0, j), :] = tiles[j]
            return tiles

        def spread(x, _):
            for c in range(7):
                tiles = tiles_of(c, x)
                low, high = (jnp.broadcast_to(ccol[c, side, pl.ds(x, 1), :], (8, NZ)) for side in range(2))
                coef[n, c, x + 1, ext(0, -1), :] = before_of(tiles[-1], low)
                coef[n, c, x + 1, ext(0, NJ), :] = after_of(tiles[0], high)
            tiles, up, down = (
                [prep_pore[x + dx, pl.ds(j, 8, stride=NJ), :] for j in range(NJ)] for dx in (1, 0, 2)
            )
            low, high = (jnp.broadcast_to(pcol[n, side, 0, pl.ds(x, 1), :], (8, NZ)) for side in range(2))
            ring = [before_of(tiles[-1], low), *tiles, after_of(tiles[0], high)]
            sums = around(ring, up, down)
            for j in range(NJ):
                perm = crep[KK, x + 1, pl.ds(j, 8, stride=NJ), :]
                coef[n, KK, x + 1, ext(0, j), :] = perm * (sums[j] - 6.0 * tiles[j])
            return 0

        lax.fori_loop(0, NX, spread, 0, unroll=2)
        for c in range(7):
            tiles_of(c, -1)
            tiles_of(c, NX)

    def right_sides(st, par, n):
        source = meta_in[st, n]
        cell = meta_in[st, 3] - (NJ * squarter + base_cell).astype(F32)

        def row(x, reach):
            tiles = [wide(st, par, x, f, reach) for f in range(2)]
            for p in range(NJ + 2 * reach):
                j = p - reach
                at = ext(0, j)
                mine = cell == jnp.asarray(x * (ngy * NY) + j).astype(F32)
                term = jnp.where(mine, source, 0.0)
                right[st, x + 1, at, :] = coef[n, RPC, x + 1, at, :] * tiles[0][p] + coef[n, IP, x + 1, at, :] * term
                right[st, x + 1, ext(1, j), :] = coef[n, RTC, x + 1, at, :] * tiles[1][p]

        def inner(x, _):
            row(x, 1)
            return 0

        lax.fori_loop(0, NX, inner, 0, unroll=2)
        row(-1, 0)
        row(NX, 0)

    def add_gradient(st, par, n):
        weight = meta_in[st, 4]

        def row(x, _):
            for j in range(NJ):
                at = pl.ds(j * 8, 8)
                gacc[x, at, :] += coef[n, KK, x + 1, ext(0, j), :] * (weight * state[st, par, x + 2, core(0, j), :])
            return 0

        lax.fori_loop(0, NX, row, 0, unroll=2)

    def swap_out(k):
        return pltpu.make_async_remote_copy(
            src_ref=outst.at[:, pl.ds(k * NY, NY), :],
            dst_ref=out_ref.at[k // NO, k % NO],
            send_sem=osend.at[k],
            recv_sem=orecv.at[k],
            device_id=partner,
            device_id_type=MESH,
        )

    def keep_out(k):
        return pltpu.make_async_copy(
            outst.at[:, pl.ds(k * NY, NY), :], out_ref.at[k // NO, k % NO], orecv.at[k]
        )

    def finish(st):
        def row(x, _):
            for f in range(2):
                for j in range(NJ):
                    outst[x, pl.ds((f * NO + st * SO) * NY + j, 8, stride=NJ), :] = state[
                        st, ROUNDS % 2, x + 2, core(f, j), :
                    ]
            return 0

        lax.fori_loop(0, NX, row, 0)

        @pl.when(moves)
        def _():
            for k in streams_obs(st):
                swap_out(k).start()

        @pl.when(stays)
        def _():
            for k in streams_obs(st):
                keep_out(k).start()

    def round_of(st, r):
        n, par = NS - 1 - r // 2, r % 2
        wait_halos(st, par)
        if r > 0:
            wait_sent(st, 1 - par)
        fill_edges(st, par)
        if r % 2 == 0:
            right_sides(st, par, n)
        first_sweep(st, par, n)
        second_sweep(st, par, n, r == ROUNDS - 1)
        if r < ROUNDS - 1:
            start_halos(st, 1 - par)
        else:
            finish(st)
        if r % 2 == 1:
            add_gradient(st, 1 - par, n)

    gacc[...] = jnp.zeros(gacc.shape, F32)
    plan = PLAN
    todo = {
        "send": send_saved, "forward": forward, "prepare": prepare, "complete": complete, "set_up": set_up,
    }

    def do(when):
        for what, n in plan.get(when, ()):
            todo[what](n)

    do("start")

    @pl.when(moves)
    def _():
        send_meta().wait()

    for r in range(ROUNDS + LAG * (ST - 1)):
        for st in range(ST):
            if 0 <= r - LAG * st < ROUNDS:
                round_of(st, r - LAG * st)
            do((r, st))
    for st in range(ST):
        wait_sent(st, (ROUNDS - 1) % 2)

    for x in range(NX):
        for j in range(NJ):
            total = gacc[x, pl.ds(j * 8, 8), :]
            for o in range(1, SO):
                total = total + pltpu.roll(gacc[x, pl.ds(j * 8, 8), :], NQ * o, 0)
            gsum[x, pl.ds(j, 8, stride=NJ), :] = total
    for h in range(2):
        whole = [gsum[x, pl.ds(h * 8, 8), :] for x in range(NX)]
        for d, tile in enumerate(regroup(whole, lane_group)):
            gpack[d, pl.ds(h * 8, 8), :] = tile

            @pl.when(jnp.logical_and(stays, obs == d))
            def _(tile=tile, h=h):
                gred[lobs, pl.ds(h * 8, 8), :] = tile

    def reduce_copy(d):
        return pltpu.make_async_remote_copy(
            src_ref=gpack.at[d],
            dst_ref=gred.at[lobs],
            send_sem=rsend.at[d],
            recv_sem=rrecv.at[lobs],
            device_id=(d, lgx, gy),
            device_id_type=MESH,
        )

    for d in range(NP):

        @pl.when(jnp.logical_not(jnp.logical_and(stays, obs == d)))
        def _(d=d):
            reduce_copy(d).start()

    for d in range(NP):

        @pl.when(jnp.logical_not(is_me(d)))
        def _(d=d):
            pltpu.make_async_remote_copy(
                src_ref=gpack.at[d],
                dst_ref=gred.at[d],
                send_sem=rsend.at[d],
                recv_sem=rrecv.at[d],
                device_id=partner,
                device_id_type=MESH,
            ).wait_recv()

    for h in range(2):
        total = gred[0, pl.ds(h * 8, 8), :]
        for d in range(1, NP):
            total = total + gred[d, pl.ds(h * 8, 8), :]
        for x in range(NX):
            turned = pltpu.roll(total, NZ - LP * x, 1) if x else total
            grad_ref[x, pl.ds(h * 8, 8), :] = turned

    for d in range(NP):

        @pl.when(jnp.logical_not(jnp.logical_and(stays, obs == d)))
        def _(d=d):
            reduce_copy(d).wait_send()

    for n in range(NS):
        for zt in range(4):

            @pl.when(jnp.logical_not(jnp.logical_and(stays, zh == zt)))
            def _(n=n, zt=zt):
                gather_copy(n, zt).wait_send()

        @pl.when(stays)
        def _(n=n):
            for d in range(NP):
                forward_copy(n, d).wait_send()

    @pl.when(moves)
    def _():
        for k in range(2 * NO):
            swap_out(k).wait()

    @pl.when(stays)
    def _():
        for k in range(2 * NO):
            keep_out(k).wait()


def local(*args):
    hbm = pl.BlockSpec(memory_space=pl.ANY)
    vmem = pl.BlockSpec(memory_space=pltpu.VMEM)
    smem = pl.BlockSpec(memory_space=pltpu.SMEM)
    dma = pltpu.SemaphoreType.DMA
    costates, gradient = pl.pallas_call(
        kernel,
        out_shape=(
            jax.ShapeDtypeStruct((2, NO, NX, NY, NZ), F32),
            jax.ShapeDtypeStruct((NX, NY, NZ), F32),
        ),
        in_specs=[hbm, hbm, hbm, hbm, hbm, vmem, smem, smem],
        out_specs=(hbm, vmem),
        scratch_shapes=[
            pltpu.VMEM((NS, 4, NX, NY, LP), F32),
            pltpu.VMEM((NS, 64, NZ), F32),
            pltpu.VMEM((NS, NP, 64, NZ), F32),
            pltpu.VMEM((NX, 2 * NO * NY, NZ), F32),
            pltpu.VMEM((ST, 5, 8, NZ), F32),
            pltpu.VMEM((ST, 5, 8, NZ), F32),
            pltpu.VMEM((ST, 2, NX + 4, ROWS, NZ), F32),
            pltpu.VMEM((ST, NX + 2, 2 * NE * 8, NZ), F32),
            pltpu.VMEM((ST, NX + 2, 2, 4, 8, NZ), F32),
            pltpu.VMEM((ST, 2, 2, 2, XG * 8, NZ), F32),
            pltpu.VMEM((ST, 2, 2, 2, XG * 8, NZ), F32),
            pltpu.VMEM((ST, 2, 4, 8, NZ), F32),
            pltpu.VMEM((NS, 8, NX + 2, NE * 8, NZ), F32),
            pltpu.VMEM((8, NX + 2, SO * NY, NZ), F32),
            pltpu.VMEM((7, 2, 8, NZ), F32),
            pltpu.VMEM((NX + 2, SO * NY, NZ), F32),
            pltpu.VMEM((NS, 4, NX * NY, NZ), F32),
            pltpu.VMEM((NS, 2, 4, 8, NZ), F32),
            pltpu.VMEM((NS, 2, 4, NY, NZ), F32),
            pltpu.VMEM((NS, 2, 4, 8, NZ), F32),
            pltpu.VMEM((ST, NX + 2, 2 * NE * 8, NZ), F32),
            pltpu.VMEM((NX, NJ * 8, NZ), F32),
            pltpu.VMEM((NX, 8 * NJ, NZ), F32),
            pltpu.VMEM((NP, NY, NZ), F32),
            pltpu.VMEM((NP, NY, NZ), F32),
            pltpu.VMEM((NX, 2 * NO * NY, NZ), F32),
            dma((NS, 4)),
            dma((NS, 4)),
            dma((NS, NP)),
            dma((NS, NP)),
            dma((2 * NO,)),
            dma((2 * NO,)),
            dma((2,)),
            dma((ST, 2, 4)),
            dma((ST, 2, 4)),
            dma((ST, 2, 4)),
            dma((ST, 2, 4)),
            dma((NS, 4)),
            dma((NS, 4)),
            dma((2 * NO,)),
            dma((2 * NO,)),
            dma((NP,)),
            dma((NP,)),
        ],
        compiler_params=pltpu.CompilerParams(
            collective_id=0, has_side_effects=True, vmem_limit_bytes=67043328
        ),
    )(*args)
    return costates, gradient[:, :, :LP]


def solution(mesh):
    return jax.shard_map(
        local,
        mesh=mesh,
        in_specs=(
            P(None, "obs", "gx", "gy", None),
            P(None, "gx", "gy", "obs"),
            P(None, "gx", "gy", "obs"),
            P(None, "gx", "gy", "obs"),
            P(None, "gx", "gy", "obs"),
            P(None, "obs", None),
            P("obs"),
            P("obs"),
        ),
        out_specs=(P(None, "obs", "gx", "gy", None), P("gx", "gy", "obs")),
        check_vma=False,
    )
```

time: 74 us -> 69.8 us (0.943)
  Pallas kernels: 70.6 us -> 66.4 us
    pallas_call x1, Pallas kernels: 70.6 us -> 66.4 us  [local(): pl.pallas_call(kernel, out_shape=(jax.ShapeDtypeStruct((2, NO, NX, NY, NZ...]
where the time goes in v4:
time: 69.8 us; the launch traced here: 69.6 us
  Pallas kernels  66.4 us (95%)
  local copies, waits for them, and re-layouts  2.53 us (4%)
    pallas_call x1, Pallas kernels, local(): pl.pallas_call(kernel, out_shape=(jax.ShapeDtypeStruct((2, NO, NX, NY, NZ...  66.4 us
    unnamed x4, local copies, waits for them, and re-layouts  2.53 us

profile of v4, /device:TPU:1, one launch (start us, length us, event | category | flops | bytes accessed | tf_op | source)
XLA Modules:
  0.0 69.6 jit_solution(6279073532938511525)
XLA Ops:
  0.6 66.4 %shard_map.95 = (f32[2,4,8,16,128]{4,3,2,1,0:T(8,128)}, f32[8,16,128]{2,1,0:T(8,128)}) custom-call(f32[2,4,8,16,128]{4,3,2,1,0:T(8,128)} %cost_ref.1, f32[3,8,16,16]{3,2,1,0:T(8,128)} %pore_ref.1, f32[3,8,16,16]{3,2,1,0:T(8,128)} %heat_ref.1, f32[3,8,16,16]{3,2,1,0:T(8,128)} %dil_ref.1, f32[3,8,16,16]{3,2,1,0:T(8,128)} %cond_ref.1, f32[3,4,128]{2,1,0:T(4,128)} %resid_ref.1, ...), custom_call_target="tpu_custom_call" | custom-call | tf_op jit(solution)/shard_map/pallas_call | solution.py:784
  67.1 0.0 copy-start
  67.1 1.9 %copy.12 = f32[2,4,8,16,128]{4,3,2,1,0:T(8,128)} copy(f32[2,4,8,16,128]{4,3,2,1,0:T(8,128)} %get-tuple-element.8) | data formatting | bytes 1048576
  69.0 0.0 copy-done
  69.0 0.6 copy.13
Async XLA Ops:
  67.1 1.9 %copy-start = (f32[8,16,128]{2,1,0:T(8,128)S(1)}, f32[8,16,128]{2,1,0:T(8,128)}, u32[]{:S(2)}) copy-start(f32[8,16,128]{2,1,0:T(8,128)} %get-tuple-element.5) | copy-start | bytes 196612

commit v5 on v4

--- a/solution.py
+++ b/solution.py
@@ -11,7 +11,7 @@
 F32 = jnp.float32
 ITERS = 4
 LAG = 0
-UNROLL = 4
+UNROLL = 8
 NX, NY, NZ = 8, 16, 128
 NS = 3
 NO = 4
@@ -31,11 +31,11 @@
 
 PLAN = {
     "start": (("forward", 2), ("send", 1), ("prepare", 2), ("set_up", 0), ("set_up", 1), ("complete", 2)),
-    (0, 0): (("forward", 1),),
-    (1, 0): (("prepare", 1),),
-    (1, 1): (("complete", 1), ("send", 0)),
-    (2, 1): (("forward", 0),),
-    (3, 0): (("prepare", 0),),
+    (0, 0): (("forward", 1), ("send", 0)),
+    (0, 1): (("prepare", 1),),
+    (1, 0): (("forward", 0),),
+    (1, 1): (("complete", 1),),
+    (2, 1): (("prepare", 0),),
     (3, 1): (("complete", 0),),
 }
 

time: 69.8 us -> 63.9 us (0.915)
  the two profiles are of different devices: /device:TPU:1 before, /device:TPU:41 now
where the time goes in v5:
time: 63.9 us; the launch traced here: 63.8 us
  Pallas kernels  60.6 us (95%)
  local copies, waits for them, and re-layouts  2.53 us (4%)
  between operations  0.65 us (1%)
    pallas_call x1, Pallas kernels, local(): pl.pallas_call(kernel, out_shape=(jax.ShapeDtypeStruct((2, NO, NX, NY, NZ...  60.6 us
    unnamed x4, local copies, waits for them, and re-layouts  2.53 us

profile of v5, /device:TPU:41, one launch (start us, length us, event | category | flops | bytes accessed | tf_op | source)
XLA Modules:
  0.0 63.8 jit_solution(6019379113883526144)
XLA Ops:
  0.6 60.6 %shard_map.95 = (f32[2,4,8,16,128]{4,3,2,1,0:T(8,128)}, f32[8,16,128]{2,1,0:T(8,128)}) custom-call(f32[2,4,8,16,128]{4,3,2,1,0:T(8,128)} %cost_ref.1, f32[3,8,16,16]{3,2,1,0:T(8,128)} %pore_ref.1, f32[3,8,16,16]{3,2,1,0:T(8,128)} %heat_ref.1, f32[3,8,16,16]{3,2,1,0:T(8,128)} %dil_ref.1, f32[3,8,16,16]{3,2,1,0:T(8,128)} %cond_ref.1, f32[3,4,128]{2,1,0:T(4,128)} %resid_ref.1, ...), custom_call_target="tpu_custom_call" | custom-call | tf_op jit(solution)/shard_map/pallas_call | solution.py:784
  61.2 0.0 copy-start
  61.2 1.9 %copy.12 = f32[2,4,8,16,128]{4,3,2,1,0:T(8,128)} copy(f32[2,4,8,16,128]{4,3,2,1,0:T(8,128)} %get-tuple-element.8) | data formatting | bytes 1048576
  63.1 0.0 copy-done
  63.1 0.6 copy.13
Async XLA Ops:
  61.2 1.9 %copy-start = (f32[8,16,128]{2,1,0:T(8,128)S(1)}, f32[8,16,128]{2,1,0:T(8,128)}, u32[]{:S(2)}) copy-start(f32[8,16,128]{2,1,0:T(8,128)} %get-tuple-element.5) | copy-start | bytes 196612

commit v6 on v5

--- a/solution.py
+++ b/solution.py
@@ -32,8 +32,7 @@
 PLAN = {
     "start": (("forward", 2), ("send", 1), ("prepare", 2), ("set_up", 0), ("set_up", 1), ("complete", 2)),
     (0, 0): (("forward", 1), ("send", 0)),
-    (0, 1): (("prepare", 1),),
-    (1, 0): (("forward", 0),),
+    (1, 0): (("prepare", 1), ("forward", 0)),
     (1, 1): (("complete", 1),),
     (2, 1): (("prepare", 0),),
     (3, 1): (("complete", 0),),
@@ -666,7 +665,7 @@
         second_sweep(st, par, n, r == ROUNDS - 1)
         if r < ROUNDS - 1:
             start_halos(st, 1 - par)
-        else:
+        elif st < ST - 1:
             finish(st)
         if r % 2 == 1:
             add_gradient(st, 1 - par, n)
@@ -692,9 +691,6 @@
             if 0 <= r - LAG * st < ROUNDS:
                 round_of(st, r - LAG * st)
             do((r, st))
-    for st in range(ST):
-        wait_sent(st, (ROUNDS - 1) % 2)
-
     for x in range(NX):
         for j in range(NJ):
             total = gacc[x, pl.ds(j * 8, 8), :]
@@ -725,6 +721,10 @@
         @pl.when(jnp.logical_not(jnp.logical_and(stays, obs == d)))
         def _(d=d):
             reduce_copy(d).start()
+
+    finish(ST - 1)
+    for st in range(ST):
+        wait_sent(st, (ROUNDS - 1) % 2)
 
     for d in range(NP):
 

time: 63.9 us -> 61.8 us (0.967)
  the two profiles are of different devices: /device:TPU:41 before, /device:TPU:1 now
where the time goes in v6:
time: 61.8 us; the launch traced here: 61.6 us
  Pallas kernels  58.4 us (94%)
  local copies, waits for them, and re-layouts  2.53 us (4%)
  between operations  0.65 us (1%)
    pallas_call x1, Pallas kernels, local(): pl.pallas_call(kernel, out_shape=(jax.ShapeDtypeStruct((2, NO, NX, NY, NZ...  58.4 us
    unnamed x4, local copies, waits for them, and re-layouts  2.53 us

profile of v6, /device:TPU:1, one launch (start us, length us, event | category | flops | bytes accessed | tf_op | source)
XLA Modules:
  0.0 61.6 jit_solution(7255924358112620088)
XLA Ops:
  0.6 58.4 %shard_map.95 = (f32[2,4,8,16,128]{4,3,2,1,0:T(8,128)}, f32[8,16,128]{2,1,0:T(8,128)}) custom-call(f32[2,4,8,16,128]{4,3,2,1,0:T(8,128)} %cost_ref.1, f32[3,8,16,16]{3,2,1,0:T(8,128)} %pore_ref.1, f32[3,8,16,16]{3,2,1,0:T(8,128)} %heat_ref.1, f32[3,8,16,16]{3,2,1,0:T(8,128)} %dil_ref.1, f32[3,8,16,16]{3,2,1,0:T(8,128)} %cond_ref.1, f32[3,4,128]{2,1,0:T(4,128)} %resid_ref.1, ...), custom_call_target="tpu_custom_call" | custom-call | tf_op jit(solution)/shard_map/pallas_call | solution.py:784
  59.1 0.0 copy-start
  59.1 1.9 %copy.12 = f32[2,4,8,16,128]{4,3,2,1,0:T(8,128)} copy(f32[2,4,8,16,128]{4,3,2,1,0:T(8,128)} %get-tuple-element.8) | data formatting | bytes 1048576
  61.0 0.0 copy-done
  61.0 0.6 %copy.13 = f32[8,16,16]{2,1,0:T(8,128)} copy(f32[8,16,16]{2,1,0:T(8,128)S(1)} %bitcast.1) | data formatting | bytes 16384
Async XLA Ops:
  59.1 1.9 %copy-start = (f32[8,16,128]{2,1,0:T(8,128)S(1)}, f32[8,16,128]{2,1,0:T(8,128)}, u32[]{:S(2)}) copy-start(f32[8,16,128]{2,1,0:T(8,128)} %get-tuple-element.5) | copy-start | bytes 196612
